TPU v7x, 256 devices: a whole 4x4x8 slice. The times are simulated.
256 devices in a mesh: row: 64 (over x, z_lo, y, core), col: 4 (over z_hi).
Axes of the slice: x: 4, y: 4, z: 8 (z_hi: 4, z_lo: 2; z = z_hi * 2 + z_lo), core: 2. Of those that a mesh axis runs over, the one named last changes fastest.
Arguments:
- fields: float32 [4, 128, 512, 512], P(None, 'row', None, 'col'), may hold values from -6 to 6
- diffusivity: float32 [4], replicated, may hold values from 0.05 to 0.3
- records: float32 [6, 2097152], P(None, ('row', 'col')), may hold values from -6 to 6
- response_time: float32 [2097152], P(('row', 'col')), may hold values from 0.5 to 4
- cell_index: int32 [2097152], P(('row', 'col')), may hold values from 0 to 131071
- counts: int32 [256], P(('row', 'col')), may hold values from 4096 to 8192, as said below
- destination: int32 [2097152], P(('row', 'col')), may hold values from 0 to 4, as said below
- slot: int32 [2097152], P(('row', 'col')), may hold values from 0 to 255, as said below
Outputs:
- tendency: float32 [4, 128, 512, 512], P(None, 'row', None, 'col')
- kept: float32 [6, 2097152], P(None, ('row', 'col'))
- arrivals: float32 [4, 6, 65536], P(None, None, ('row', 'col'))
Inputs may be any that keep to these rules, and one draw needn't show every extreme that they name: `counts`: both wall rows of pencils are full. `destination`: only live particles leave; none leaves row index 0 downward or row index 63 upward. For each pencil and direction the leaving particles' slots are distinct; pencil 0 sends exactly 256 particles toward col index + 1; slot is 0 for particles that stay.
All inputs are finite; a program needn't handle non-finite values.
Results may differ from a plain program's by a relative error of at most 0.00009.
Values sent between devices are 32-bit elements; how exact they have to be, the bound alone decides.
A program may use at most 192 MiB of HBM per device.

v0:
```python
import math

import jax
import jax.numpy as jnp
from jax import lax
from jax.sharding import PartitionSpec as P

PART_DEV = 8192
MIG = 256


time_step = 0.2
coupling = 0.5
stretch = 1.5


def shifted(value, axis, steps):
    count = lax.axis_size(axis)
    first, last = (max(0, -steps), min(count, count - steps))
    return lax.ppermute(value, axis, [(source, source + steps) for source in range(first, last)])


def from_behind(block, axis, distance):
    devices = range(lax.axis_size(axis))
    route = [((i - distance) % len(devices), i) for i in devices]
    return lax.ppermute(block, axis, route)


def periodic_compact(points):
    index = jnp.arange(points, dtype=jnp.int32)
    offset = (index[None, :] - index[:, None]) % points
    lhs = jnp.where(offset == 0, 1.0, 0.0) + jnp.where(
        (offset == 1) | (offset == points - 1), 1.0 / 3.0, 0.0
    )
    rhs = jnp.where(offset == 1, 7.0 / 9.0, 0.0) - jnp.where(offset == points - 1, 7.0 / 9.0, 0.0)
    rhs = (
        rhs
        + jnp.where(offset == 2, 1.0 / 36.0, 0.0)
        - jnp.where(offset == points - 2, 1.0 / 36.0, 0.0)
    )
    factor = jnp.linalg.cholesky(lhs.astype(jnp.float32))
    return jax.scipy.linalg.cho_solve((factor, True), rhs.astype(jnp.float32))


def wall_compact(points):
    index = jnp.arange(points, dtype=jnp.int32)
    first = index == 0
    final = index == points - 1
    near = (index == 1) | (index == points - 2)
    lower = jnp.where(first, 0.0, jnp.where(final, 2.0, jnp.where(near, 0.25, 1.0 / 3.0))).astype(
        jnp.float32
    )
    upper = jnp.where(final, 0.0, jnp.where(first, 2.0, jnp.where(near, 0.25, 1.0 / 3.0))).astype(
        jnp.float32
    )
    middle = jnp.ones((points,), jnp.float32)
    offset = index[None, :] - index[:, None]
    inner = jnp.where(offset == 1, 7.0 / 9.0, 0.0) - jnp.where(offset == -1, 7.0 / 9.0, 0.0)
    inner = (
        inner + jnp.where(offset == 2, 1.0 / 36.0, 0.0) - jnp.where(offset == -2, 1.0 / 36.0, 0.0)
    )
    padde_rows = jnp.where(offset == 1, 0.75, 0.0) - jnp.where(offset == -1, 0.75, 0.0)
    top_row = (
        jnp.where(offset == 0, -2.5, 0.0)
        + jnp.where(offset == 1, 2.0, 0.0)
        + jnp.where(offset == 2, 0.5, 0.0)
    )
    end_row = (
        jnp.where(offset == 0, 2.5, 0.0)
        - jnp.where(offset == -1, 2.0, 0.0)
        - jnp.where(offset == -2, 0.5, 0.0)
    )
    rhs = jnp.where(
        first[:, None],
        top_row,
        jnp.where(final[:, None], end_row, jnp.where(near[:, None], padde_rows, inner)),
    )
    solved = lax.linalg.tridiagonal_solve(lower, middle, upper, rhs.astype(jnp.float32))
    coord = -1.0 + 2.0 * index.astype(jnp.float32) / (points - 1)
    slope = stretch * (1.0 - jnp.tanh(stretch * coord) ** 2) / math.tanh(stretch)
    return solved / slope[:, None]


def spectral_matrix(points):
    index = jnp.arange(points, dtype=jnp.int32)
    offset = index[:, None] - index[None, :]
    parity = (1 - 2 * (offset % 2)).astype(jnp.float32)
    angle = math.pi * offset.astype(jnp.float32) / points
    safe_angle = jnp.where(offset == 0, 1.0, angle)
    value = math.pi / points * parity * jnp.cos(safe_angle) / jnp.sin(safe_angle)
    return jnp.where(offset == 0, 0.0, value)


def spanwise_terms(pencil_data, viscous):
    highest = lax.Precision.HIGHEST
    deriv_z = spectral_matrix(pencil_data.shape[3])
    second_z = jnp.dot(deriv_z, deriv_z, precision=highest)
    along_z = jnp.einsum("ij,cabj->cabi", deriv_z, pencil_data, precision=highest)
    curve_z = jnp.einsum("ij,cabj->cabi", second_z, pencil_data, precision=highest)
    return -pencil_data[2] * along_z + viscous * curve_z


def on_device(fields, diffusivity, records, response_time, cell_index, counts, destination, slot):
    highest = lax.Precision.HIGHEST
    viscous = diffusivity[:, None, None, None]
    planes = fields.shape[2]
    deriv_x = periodic_compact(planes)
    second_x = jnp.dot(deriv_x, deriv_x, precision=highest)
    along_x = jnp.einsum("ij,cyjz->cyiz", deriv_x, fields, precision=highest)
    curve_x = jnp.einsum("ij,cyjz->cyiz", second_x, fields, precision=highest)
    partial_x = -fields[0] * along_x + viscous * curve_x
    local = jnp.arange(PART_DEV, dtype=jnp.int32)
    live = local < counts[0]
    flat_speed = fields[0:3].reshape(3, -1)
    fluid = jnp.take(flat_speed, cell_index, axis=1)
    drag = (fluid - records[3:6]) / response_time
    velocity = records[3:6] + time_step * drag
    moved_pos = records[0:3] + time_step * velocity
    moved = jnp.concatenate([moved_pos, velocity], axis=0)
    force = jnp.where(live[None, :], -coupling * drag, 0.0)
    deposit = (
        jnp.zeros_like(flat_speed)
        .at[:, cell_index]
        .add(force)
        .reshape(3, fields.shape[1], fields.shape[2], fields.shape[3])
    )
    partial_x = partial_x.at[0:3].add(deposit)
    normal_pencil = lax.all_to_all(fields, "row", split_axis=2, concat_axis=1, tiled=True)
    deriv_y = wall_compact(normal_pencil.shape[1])
    second_y = jnp.dot(deriv_y, deriv_y, precision=highest)
    along_y = jnp.einsum("ij,cjxz->cixz", deriv_y, normal_pencil, precision=highest)
    curve_y = jnp.einsum("ij,cjxz->cixz", second_y, normal_pencil, precision=highest)
    partial_y = -normal_pencil[1] * along_y + viscous * curve_y
    span_pencil = lax.all_to_all(normal_pencil, "col", split_axis=1, concat_axis=3, tiled=True)
    partial_z = spanwise_terms(span_pencil, viscous)
    partial_y = partial_y + lax.all_to_all(
        partial_z, "col", split_axis=3, concat_axis=1, tiled=True
    )
    tendency = partial_x + lax.all_to_all(partial_y, "row", split_axis=1, concat_axis=2, tiled=True)
    staying = live & (destination == 0)
    kept = jnp.where(staying[None, :], moved, 0.0)
    leaving = live & (destination > 0)
    target = jnp.where(leaving, (destination - 1) * MIG + slot, 4 * MIG)
    outgoing = (
        jnp.zeros((6, 4 * MIG + 1), jnp.float32)
        .at[:, target]
        .add(jnp.where(leaving[None, :], moved, 0.0))
    )
    outgoing = outgoing[:, : 4 * MIG].reshape(6, 4, MIG)
    received = []
    for direction, offset in ((0, 1), (1, -1)):
        received.append(shifted(outgoing[:, direction], "row", offset))
    for direction, offset in ((2, 1), (3, -1)):
        received.append(from_behind(outgoing[:, direction], "col", offset))
    arrivals = jnp.stack(received, axis=0)
    return (tendency, kept, arrivals)


def solution(mesh):
    return jax.shard_map(
        on_device,
        mesh=mesh,
        in_specs=(
            P(None, "row", None, "col"),
            P(),
            P(None, ("row", "col")),
            P(("row", "col")),
            P(("row", "col")),
            P(("row", "col")),
            P(("row", "col")),
            P(("row", "col")),
        ),
        out_specs=(
            P(None, "row", None, "col"),
            P(None, ("row", "col")),
            P(None, None, ("row", "col")),
        ),
        check_vma=False,
    )
```

profile of v0, /device:TPU:2, one launch (start us, length us, event | category | flops | bytes accessed | tf_op | source)
XLA Modules:
  0.0 1093.2 jit_solution(8864007310958328743)
XLA Ops:
  0.6 4.3 copy.115
  4.9 9.6 all-to-all-start
  15.9 30.5 %copy.111 = f32[3,2,512,128]{0,3,2,1:T(8,128)} copy(f32[3,2,512,128]{3,2,1,0:T(8,128)S(1)} %slice-done) | data formatting | bytes 3145728 | tf_op jit(solution)/shard_map/slice | solution.py:114
  46.4 118.5 %gather_fusion = f32[8192,3]{1,0:T(8,128)} fusion(f32[3,131072]{0,1:T(8,128)} %bitcast.277, s32[8192]{0:T(1024)S(1)} %get-tuple-element.480), kind=kCustom, calls=%fused_computation | custom fusion | bytes 229376 | tf_op jit(solution)/shard_map/jit(_take)/gather | solution.py:115
  172.1 52.0 %scatter_custom_fusion.1 = f32[6,1025]{0,1:T(8,128)S(1)} fusion(s32[8192]{0:T(1024)S(1)} %compare_select_fusion, f32[8192,6]{1,0:T(8,128)} %copy.126, f32[]{:T(128)} %constant.319.clone.1), kind=kCustom, calls=%fused_computation.317 | custom fusion | flops 49152 | bytes 25112 | tf_op jit(solution)/shard_map/scatter-add | solution.py:147
  224.2 4.9 collective-permute-start.3
  230.6 4.9 collective-permute-start.1
  240.7 194.9 %while.34 = (s32[]{:T(128)}, f32[]{:T(128)}, f32[128]{0:T(128)S(1)}, f32[3,32]{1,0:T(4,128)S(1)}, f32[3,32,128]{2,1,0:T(8,128)S(1)}, /*index=5*/f32[3,32]{1,0:T(...) while((s32[]{:T(128)}, f32[]{:T(128)}, ...), condition=%wide.region_10.11_spmd, body=%wide.region_9.10_spmd.sunk | while | flops 12417 | bytes 103669 | solution.py:78
  284.5 20.2 %fusion.526 = (f32[128]{0:T(128)S(1)}, f32[128]{0:T(128)S(1)}, f32[128]{0:T(128)S(1)}, f32[128]{0:T(128)S(1)}, f32[128]{0:T(128)S(1)}, /*index=5*/f32[128]{0:T(1...) fusion(f32[3,32,128]{2,1,0:T(8,128)S(1)} %get-tuple-element.112, ...), kind=kLoop, calls=%fused_computation.44.clone.1 | loop fusion | flops 12288 | bytes 33664 | tf_op jit(solution)/shard_map/while/body/eval_jaxpr/div | solution.py:78
  349.3 20.2 %fusion.526 = (f32[128]{0:T(128)S(1)}, f32[128]{0:T(128)S(1)}, f32[128]{0:T(128)S(1)}, f32[128]{0:T(128)S(1)}, f32[128]{0:T(128)S(1)}, /*index=5*/f32[128]{0:T(1...) fusion(f32[3,32,128]{2,1,0:T(8,128)S(1)} %get-tuple-element.112, ...), kind=kLoop, calls=%fused_computation.44.clone.1 | loop fusion | flops 12288 | bytes 33664 | tf_op jit(solution)/shard_map/while/body/eval_jaxpr/div | solution.py:78
  414.1 20.2 %fusion.526 = (f32[128]{0:T(128)S(1)}, f32[128]{0:T(128)S(1)}, f32[128]{0:T(128)S(1)}, f32[128]{0:T(128)S(1)}, f32[128]{0:T(128)S(1)}, /*index=5*/f32[128]{0:T(1...) fusion(f32[3,32,128]{2,1,0:T(8,128)S(1)} %get-tuple-element.112, ...), kind=kLoop, calls=%fused_computation.44.clone.1 | loop fusion | flops 12288 | bytes 33664 | tf_op jit(solution)/shard_map/while/body/eval_jaxpr/div | solution.py:78
  439.3 11.7 %cholesky.104 = f32[128,128]{1,0:T(8,128)S(1)} custom-call(f32[128,128]{1,0:T(8,128)S(1)} %cholesky.266), custom_call_target="Cholesky" | custom-call | tf_op jit(solution)/shard_map/jit(cholesky)/cholesky | solution.py:41
  451.2 9.8 custom-call.34
  461.7 11.7 %cholesky.217 = f32[128,128]{1,0:T(8,128)S(1)} custom-call(f32[128,128]{1,0:T(8,128)S(1)} %cholesky.270), custom_call_target="Cholesky" | custom-call | tf_op jit(solution)/shard_map/jit(cholesky)/cholesky | solution.py:41
  473.4 10.0 custom-call.35
  484.1 11.7 %cholesky.238 = f32[128,128]{1,0:T(8,128)S(1)} custom-call(f32[128,128]{1,0:T(8,128)S(1)} %cholesky.275), custom_call_target="Cholesky" | custom-call | tf_op jit(solution)/shard_map/jit(cholesky)/cholesky | solution.py:41
  495.8 9.8 custom-call.36
  506.2 11.7 %cholesky.255 = f32[128,128]{1,0:T(8,128)S(1)} custom-call(f32[128,128]{1,0:T(8,128)S(1)} %convolution_subtract_fusion.8), custom_call_target="Cholesky" | custom-call | tf_op jit(solution)/shard_map/jit(cholesky)/cholesky | solution.py:41
  558.4 19.7 %fusion.304 = (f32[128]{0:T(128)S(1)}, f32[128]{0:T(128)S(1)}, f32[128]{0:T(128)S(1)}, f32[128]{0:T(128)S(1)}, f32[128]{0:T(128)S(1)}, /*index=5*/f32[128]{0:T(1...) fusion(f32[128,128]{1,0:T(8,128)S(1)} %select_select_fusion.1, ...), kind=kLoop, calls=%fused_computation.488 | loop fusion | flops 11904 | bytes 32504 | tf_op jit(solution)/shard_map/eval_jaxpr/div | solution.py:78
  582.3 6.5 sort
  588.9 65.7 %while.35 = (s32[]{:T(128)}, f32[128]{0:T(128)S(1)}, f32[3,32,128]{2,1,0:T(8,128)S(1)}, f32[3,32,128]{2,1,0:T(8,128)S(1)}, f32[3,32]{1,0:T(4,128)S(1)}, /*index=...) while((s32[]{:T(128)}, f32[128]{0:T(128)S(1)}, ...), condition=%wide.region_12.13_spmd, body=%wide.region_11.12_spmd.sunk | while | flops 8226 | bytes 101341 | solution.py:78
  590.3 20.3 %fusion.529 = (f32[128]{0:T(128)S(1)}, f32[128]{0:T(128)S(1)}, f32[128]{0:T(128)S(1)}, f32[128]{0:T(128)S(1)}, f32[128]{0:T(128)S(1)}, /*index=5*/f32[128]{0:T(1...) fusion(f32[3,32,128]{2,1,0:T(8,128)S(1)} %get-tuple-element.123, ...), kind=kLoop, calls=%fused_computation.172.clone.1 | loop fusion | flops 8192 | bytes 33536 | tf_op jit(solution)/shard_map/while/body/eval_jaxpr/sub | solution.py:78
  612.3 20.3 %fusion.529 = (f32[128]{0:T(128)S(1)}, f32[128]{0:T(128)S(1)}, f32[128]{0:T(128)S(1)}, f32[128]{0:T(128)S(1)}, f32[128]{0:T(128)S(1)}, /*index=5*/f32[128]{0:T(1...) fusion(f32[3,32,128]{2,1,0:T(8,128)S(1)} %get-tuple-element.123, ...), kind=kLoop, calls=%fused_computation.172.clone.1 | loop fusion | flops 8192 | bytes 33536 | tf_op jit(solution)/shard_map/while/body/eval_jaxpr/sub | solution.py:78
  634.2 20.3 %fusion.529 = (f32[128]{0:T(128)S(1)}, f32[128]{0:T(128)S(1)}, f32[128]{0:T(128)S(1)}, f32[128]{0:T(128)S(1)}, f32[128]{0:T(128)S(1)}, /*index=5*/f32[128]{0:T(1...) fusion(f32[3,32,128]{2,1,0:T(8,128)S(1)} %get-tuple-element.123, ...), kind=kLoop, calls=%fused_computation.172.clone.1 | loop fusion | flops 8192 | bytes 33536 | tf_op jit(solution)/shard_map/while/body/eval_jaxpr/sub | solution.py:78
  656.4 3.3 fusion.368
  659.6 3.3 fusion.367
  678.7 3.3 fusion.361
  682.0 7.0 convolution_bitcast_fusion
  694.4 6.5 all-to-all-start.1
  700.9 10.2 while.36
  711.2 23.3 %all-to-all-done.1 = f32[4,128,8,128]{3,2,0,1:T(8,128)} async-done(((f32[4,128,8,128]{3,2,0,1:T(8,128)}), f32[4,128,8,128]{3,2,0,1:T(8,128)}, u32[]{:S(2)}, u32[]{:S(2)}) %all-to-all-start.1) | async-done | bytes 2097184 | tf_op jit(solution)/shard_map/all_to_all | solution.py:134
  734.6 4.3 copy.121
  745.3 3.5 fusion.493
  748.8 9.0 bitcast_add_fusion.2
  757.9 8.4 copy.122
  766.3 7.3 reshape.572
  773.6 18.9 %all-to-all-start.2 = ((f32[4,1,131072]{2,1,0:T(1,128)}), f32[4,1,131072]{2,1,0:T(1,128)}, u32[]{:S(2)}, u32[]{:S(2)}) async-start(f32[4,1,131072]{2,1,0:T(1,128)} %reshape.572), calls=%async_computation.2 | async-start | bytes 4194304 | tf_op jit(solution)/shard_map/all_to_all | solution.py:136
  795.1 40.7 %custom-call.37 = f32[4,128,128]{1,2,0:T(8,128)} custom-call(f32[4,128,128]{2,1,0:T(8,128)} %get-tuple-element.177), custom_call_target="InvertDiagBlocksLowerTriangular" | custom-call | tf_op jit(solution)/shard_map/jit(_cho_solve)/triangular_solve | solution.py:42
  838.5 121.9 %scatter_custom_fusion = f32[3,131072]{0,1:T(8,128)} fusion(s32[8192]{0:T(1024)} %get-tuple-element.196, f32[]{:T(128)} %constant.319.clone.1, f32[8192,3]{1,0:T(8,128)} %copy.113, s32[8192]{0:T(1024)S(1)} %broadcast_clamp_fusion), kind=kCustom, calls=%fused_computation.235 | custom fusion | flops 24576 | bytes 1573376 | tf_op jit(solution)/shard_map/scatter-add | solution.py:124
  960.5 36.1 %copy.138 = f32[3,2,512,128]{3,2,1,0:T(8,128)} copy(f32[3,2,512,128]{0,3,2,1:T(8,128)} %bitcast.280) | data formatting | bytes 3145728 | tf_op jit(solution)/shard_map/reshape.84
  1021.2 9.0 reduce.26
  1030.2 7.8 reshape.573
  1037.9 6.3 copy.123
  1044.2 4.5 bitcast_add_fusion.1
  1051.3 11.0 %all-to-all-start.3 = ((f32[4,128,8,128]{3,2,0,1:T(8,128)}), f32[4,128,8,128]{3,2,0,1:T(8,128)}, u32[]{:S(2)}, u32[]{:S(2)}) async-start(f32[4,128,8,128]{3,2,0,1:T(8,128)} %copy.124), calls=%async_computation.3 | async-start | bytes 4194304 | tf_op jit(solution)/shard_map/all_to_all | solution.py:139
  1069.3 3.6 fusion.492
  1072.9 3.7 bitcast_add_fusion.3
  1078.5 11.2 %all-to-all-done.3 = f32[4,128,8,128]{3,2,0,1:T(8,128)} async-done(((f32[4,128,8,128]{3,2,0,1:T(8,128)}), f32[4,128,8,128]{3,2,0,1:T(8,128)}, u32[]{:S(2)}, u32[]{:S(2)}) %all-to-all-start.3) | async-done | bytes 2097184 | tf_op jit(solution)/shard_map/all_to_all | solution.py:139
  (232 shorter events, 121.2 us)
Async XLA Ops:
  4.9 684.3 %all-to-all-start = ((f32[4,2,512,128]{3,0,1,2:T(4,128)}), f32[4,2,512,128]{3,0,1,2:T(4,128)}, u32[]{:S(2)}, u32[]{:S(2)}) async-start(f32[4,2,512,128]{3,0,1,2:T(4,128)} %copy.115), calls=%async_computation | async-start | bytes 4194304 | tf_op jit(solution)/shard_map/all_to_all | solution.py:128
  14.5 0.8 copy-start.10
  14.5 1.4 slice-start
  164.8 3.6 copy-start.11
  164.8 3.6 copy-start.9
  164.8 3.6 copy-start.12
  169.4 2.7 copy-start.13
  224.2 852.9 %collective-permute-start.3 = (f32[6,256]{1,0:T(8,128)S(1)}, f32[6,256]{1,0:T(8,128)}, u32[]{:S(2)}, u32[]{:S(2)}) collective-permute-start(f32[6,256]{1,0:T(8,128)S(1)} %bitcast.1864), channel_id=1, source_target_pairs={{1,0},{2,1},{3,2},{0,3},{5,4},{6,5},{7,6},{4,7},{9,8},{10,9},{11,1... | collective-permute-start | bytes 18440 | tf_op jit(solution)/shard_map/ppermute | solution.py:26
  229.8 847.3 %collective-permute-start.2 = (f32[6,256]{1,0:T(8,128)}, f32[6,256]{1,0:T(8,128)}, u32[]{:S(2)}, u32[]{:S(2)}) collective-permute-start(f32[6,256]{1,0:T(8,128)} %bitcast.568), channel_id=1, source_target_pairs={{3,0},{0,1},{1,2},{2,3},{7,4},{4,5},{5,6},{6,7},{11,8},{8,9},{9,10... | collective-permute-start | bytes 18440 | tf_op jit(solution)/shard_map/ppermute | solution.py:26
  230.6 846.5 %collective-permute-start.1 = (f32[6,256]{1,0:T(8,128)}, f32[6,256]{1,0:T(8,128)}, u32[]{:S(2)}, u32[]{:S(2)}) collective-permute-start(f32[6,256]{1,0:T(8,128)} %bitcast.566), channel_id=1, source_target_pairs={{4,0},{8,4},{12,8},{16,12},{20,16},{24,20},{28,24},{32,28},{36,32}... | collective-permute-start | bytes 18440 | tf_op jit(solution)/shard_map/ppermute | solution.py:20
  236.2 840.9 %collective-permute-start = (f32[6,256]{1,0:T(8,128)}, f32[6,256]{1,0:T(8,128)}, u32[]{:S(2)}, u32[]{:S(2)}) collective-permute-start(f32[6,256]{1,0:T(8,128)} %bitcast.564), channel_id=1, source_target_pairs={{0,4},{4,8},{8,12},{12,16},{16,20},{20,24},{24,28},{28,32},{32,36}... | collective-permute-start | bytes 18440 | tf_op jit(solution)/shard_map/ppermute | solution.py:20
  435.6 219.0 %copy-start.8 = (f32[3,32,128]{2,1,0:T(8,128)}, f32[3,32,128]{2,1,0:T(8,128)S(1)}, u32[]{:S(2)}) copy-start(f32[3,32,128]{2,1,0:T(8,128)S(1)} %get-tuple-element.164) | copy-start | bytes 147460
  694.4 6.5 copy-start.24
  694.4 40.2 %all-to-all-start.1 = ((f32[4,128,8,128]{3,2,0,1:T(8,128)}), f32[4,128,8,128]{3,2,0,1:T(8,128)}, u32[]{:S(2)}, u32[]{:S(2)}) async-start(f32[4,128,8,128]{3,2,0,1:T(8,128)} %copy.117), calls=%async_computation.1 | async-start | bytes 4194304 | tf_op jit(solution)/shard_map/all_to_all | solution.py:134
  741.9 2.2 copy-start.6
  743.7 1.6 copy-start.1
  745.3 3.5 copy-start.14
  773.6 247.1 %all-to-all-start.2 = ((f32[4,1,131072]{2,1,0:T(1,128)}), f32[4,1,131072]{2,1,0:T(1,128)}, u32[]{:S(2)}, u32[]{:S(2)}) async-start(f32[4,1,131072]{2,1,0:T(1,128)} %reshape.572), calls=%async_computation.2 | async-start | bytes 4194304 | tf_op jit(solution)/shard_map/all_to_all | solution.py:136
  960.4 51.3 %copy-start.15 = (f32[1,128]{1,0:T(1,128)S(1)}, f32[1,128]{1,0:T(1,128)}, u32[]{:S(2)}) copy-start(f32[1,128]{1,0:T(1,128)} %get-tuple-element.299) | copy-start | bytes 1540
  960.4 51.3 %copy-start.16 = (f32[1,128]{1,0:T(1,128)S(1)}, f32[1,128]{1,0:T(1,128)}, u32[]{:S(2)}) copy-start(f32[1,128]{1,0:T(1,128)} %get-tuple-element.301) | copy-start | bytes 1540
  960.4 51.3 %copy-start.17 = (f32[1,128]{1,0:T(1,128)S(1)}, f32[1,128]{1,0:T(1,128)}, u32[]{:S(2)}) copy-start(f32[1,128]{1,0:T(1,128)} %get-tuple-element.303) | copy-start | bytes 1540
  960.4 51.3 %copy-start.18 = (f32[1,128]{1,0:T(1,128)S(1)}, f32[1,128]{1,0:T(1,128)}, u32[]{:S(2)}) copy-start(f32[1,128]{1,0:T(1,128)} %get-tuple-element.305) | copy-start | bytes 1540
  960.5 51.3 %copy-start.19 = (f32[1,128]{1,0:T(1,128)S(1)}, f32[1,128]{1,0:T(1,128)}, u32[]{:S(2)}) copy-start(f32[1,128]{1,0:T(1,128)} %get-tuple-element.307) | copy-start | bytes 1540
  960.5 51.3 %copy-start.20 = (f32[1,128]{1,0:T(1,128)S(1)}, f32[1,128]{1,0:T(1,128)}, u32[]{:S(2)}) copy-start(f32[1,128]{1,0:T(1,128)} %get-tuple-element.309) | copy-start | bytes 1540
  960.5 51.3 %copy-start.21 = (f32[1,128]{1,0:T(1,128)S(1)}, f32[1,128]{1,0:T(1,128)}, u32[]{:S(2)}) copy-start(f32[1,128]{1,0:T(1,128)} %get-tuple-element.311) | copy-start | bytes 1540
  960.5 51.3 %copy-start.22 = (f32[1,128]{1,0:T(1,128)S(1)}, f32[1,128]{1,0:T(1,128)}, u32[]{:S(2)}) copy-start(f32[1,128]{1,0:T(1,128)} %get-tuple-element.313) | copy-start | bytes 1540
  960.5 51.3 %copy-start.23 = (f32[1,128]{1,0:T(1,128)S(1)}, f32[1,128]{1,0:T(1,128)}, u32[]{:S(2)}) copy-start(f32[1,128]{1,0:T(1,128)} %get-tuple-element.315) | copy-start | bytes 1540
  1012.7 1.4 copy-start.3
  1051.3 11.1 %copy-start.4 = (f32[512,512]{1,0:T(8,128)S(1)}, f32[512,512]{1,0:T(8,128)}, u32[]{:S(2)}) copy-start(f32[512,512]{1,0:T(8,128)} %copy-done.3) | copy-start | bytes 3145732
  1051.3 11.1 %copy-start.5 = (f32[128,512]{1,0:T(8,128)S(1)}, f32[128,512]{1,0:T(8,128)}, u32[]{:S(2)}) copy-start(f32[128,512]{1,0:T(8,128)} %fusion.238) | copy-start | bytes 786436
  1051.3 11.5 %copy-start.7 = (f32[4,128,128]{1,2,0:T(8,128)S(1)}, f32[4,128,128]{1,2,0:T(8,128)}, u32[]{:S(2)}) copy-start(f32[4,128,128]{1,2,0:T(8,128)} %custom-call.37) | copy-start | bytes 786436
  1051.3 38.4 %all-to-all-start.3 = ((f32[4,128,8,128]{3,2,0,1:T(8,128)}), f32[4,128,8,128]{3,2,0,1:T(8,128)}, u32[]{:S(2)}, u32[]{:S(2)}) async-start(f32[4,128,8,128]{3,2,0,1:T(8,128)} %copy.124), calls=%async_computation.3 | async-start | bytes 4194304 | tf_op jit(solution)/shard_map/all_to_all | solution.py:139
  1066.3 2.9 copy-start
  1072.9 3.7 copy-start.2
where the time goes:
time: 1110 us; the launch traced here: 1090 us
  other arithmetic  504 us (45%)
  local copies, waits for them, and re-layouts  281 us (25%)
  loops' own time  125 us (11%)
  starting transfers between devices  57.9 us (5%)
  matrix products  47.3 us (4%)
  between operations  44 us (4%)
  waiting for transfers between devices  34.6 us (3%)
    scatter-add x3, other arithmetic, on_device(): deposit = jnp.zeros_like(flat_speed).at[:, cell_index].add(force).reshape...  128 us
    another operation x2, loops' own time, wall_compact(): lax.linalg.tridiagonal_solve(lower, middle, upper, rhs.astype(jnp.float32))  125 us
    gather x2, local copies, waits for them, and re-layouts, on_device(): fluid = jnp.take(flat_speed, cell_index, axis=1)  121 us
    div x4, other arithmetic, wall_compact(): lax.linalg.tridiagonal_solve(lower, middle, upper, rhs.astype(jnp.float32))  80.3 us
    another operation x14, other arithmetic, periodic_compact(): factor = jnp.linalg.cholesky(lhs.astype(jnp.float32))  78.7 us
    sub x3, other arithmetic, wall_compact(): lax.linalg.tridiagonal_solve(lower, middle, upper, rhs.astype(jnp.float32))  61 us
    scatter-add x1, other arithmetic, on_device(): outgoing = jnp.zeros((6, 4 * MIG + 1), jnp.float32).at[:, target].add(jnp...  52 us
    another operation x15, local copies, waits for them, and re-layouts  46.3 us
  transfers between devices with their start and end apart: 8, of which 2 were waited for; matrix products, arithmetic and copies ran while one was open for 75% of the time, Pallas kernels for 0%

commit v1 on v0

v1 whole, which is shorter than its diff:
```python
import math

import jax
import jax.numpy as jnp
import numpy as np
from jax import lax
from jax.experimental import pallas as pl
from jax.experimental.pallas import tpu as pltpu
from jax.sharding import PartitionSpec as P

F32, BF16 = jnp.float32, jnp.bfloat16
NX, NY, NZ, YR, ZC = 512, 128, 512, 2, 128
PART, MIG = 8192, 256
ROWS, COLS = 64, 4
XB = NX // ROWS
CHUNK = 1024
CELLS = YR * NX
STEP, COUPLING, STRETCH = 0.2, 0.5, 1.5


def periodic_compact(n):
    eye = np.eye(n)
    up, up2 = np.roll(eye, 1, 1), np.roll(eye, 2, 1)
    lhs = eye + (up + up.T) / 3.0
    rhs = (up - up.T) * 7.0 / 9.0 + (up2 - up2.T) / 36.0
    return np.linalg.solve(lhs, rhs)


def wall_compact(n):
    lhs, rhs = np.eye(n), np.zeros((n, n))
    for j in range(1, n - 1):
        near = j in (1, n - 2)
        lhs[j, j - 1] = lhs[j, j + 1] = 0.25 if near else 1.0 / 3.0
        rhs[j, j + 1] = 0.75 if near else 7.0 / 9.0
        rhs[j, j - 1] = -rhs[j, j + 1]
        if not near:
            rhs[j, j + 2], rhs[j, j - 2] = 1.0 / 36.0, -1.0 / 36.0
    lhs[0, 1] = lhs[n - 1, n - 2] = 2.0
    rhs[0, :3] = (-2.5, 2.0, 0.5)
    rhs[n - 1, n - 3 :] = (-0.5, -2.0, 2.5)
    eta = -1.0 + 2.0 * np.arange(n) / (n - 1)
    slope = STRETCH * (1.0 - np.tanh(STRETCH * eta) ** 2) / math.tanh(STRETCH)
    return np.linalg.solve(lhs, rhs) / slope[:, None]


def spectral(n):
    offset = np.arange(n)[:, None] - np.arange(n)[None, :]
    safe = np.where(offset == 0, 1, offset)
    value = math.pi / n * (1.0 - 2.0 * (offset % 2)) / np.tan(math.pi * safe / n)
    return np.where(offset == 0, 0.0, value)


def split_np(matrix):
    high = matrix.astype(np.float32).astype(BF16)
    low = (matrix - high.astype(np.float64)).astype(np.float32).astype(BF16)
    return high, low


def split(value):
    high = value.astype(BF16)
    return high, (value - high.astype(F32)).astype(BF16)


def constants():
    dx, dy, dz = periodic_compact(NX), wall_compact(NY), spectral(NZ)
    x_row = np.concatenate([dx[:128], (dx @ dx)[:128]], 0)
    z_t = np.concatenate([dz.T[:128], (dz @ dz).T[:128]], 0)
    x_high, x_low = split_np(x_row)
    z_high, z_low = split_np(z_t)
    y_high, y_low = split_np(np.concatenate([dy, dy @ dy], 0))
    y_three = np.concatenate([y_high, y_high, y_low], 1)
    return np.stack([x_high, x_low]), y_three, np.stack([z_high, z_low])


def nt(a, b):
    return lax.dot_general(a, b, (((1,), (1,)), ((), ())), preferred_element_type=F32)


def mm(a, b):
    return jnp.dot(a, b, preferred_element_type=F32)


def particle_kernel(counts, fields, records, response, cell, dest, slot, kept, deposit, outgoing, table, spilled):
    step = pl.program_id(0)

    @pl.when(step == 0)
    def _():
        for a in range(3):
            high, low = split(fields[a].reshape(CELLS, ZC).T)
            table[pl.ds(a * ZC, ZC), :] = high
            table[pl.ds((3 + a) * ZC, ZC), :] = low
        deposit[...] = jnp.zeros_like(deposit)
        spilled[...] = jnp.zeros_like(spilled)

    index = cell[...]
    row, lane = index // ZC, index % ZC
    local = step * CHUNK + lax.broadcasted_iota(jnp.int32, (1, CHUNK), 1)
    live = local < counts[0]
    in_row = lax.broadcasted_iota(jnp.int32, (CELLS, CHUNK), 0) == row
    hot = jnp.where(in_row, 1.0, 0.0).astype(BF16)
    in_lane = lax.broadcasted_iota(jnp.int32, (ZC, CHUNK), 0) == lane
    picked = mm(table[...], hot)
    fluid = []
    for a in range(3):
        both = picked[a * ZC : (a + 1) * ZC] + picked[(3 + a) * ZC : (4 + a) * ZC]
        fluid.append(jnp.sum(jnp.where(in_lane, both, 0.0), axis=0, keepdims=True))
    fluid = jnp.concatenate(fluid, axis=0)
    speed = records[3:6, :]
    drag = (fluid - speed) / response[...]
    velocity = speed + STEP * drag
    moved = jnp.concatenate([records[0:3, :] + STEP * velocity, velocity], axis=0)
    kept[...] = jnp.where(live & (dest[...] == 0), moved, 0.0)
    force = jnp.where(live, -COUPLING * drag, 0.0)
    spread = jnp.concatenate([jnp.where(in_lane, force[a : a + 1], 0.0) for a in range(3)], axis=0)
    high, low = split(spread)
    laid = nt(hot, high) + nt(hot, low)
    for a in range(3):
        deposit[a] += laid[:, a * ZC : (a + 1) * ZC]
    leaving = live & (dest[...] > 0)
    place = jnp.where(leaving, (dest[...] - 1) * 2 + slot[...] // 128, 8)
    in_half = lax.broadcasted_iota(jnp.int32, (8, CHUNK), 0) == place
    in_slot = lax.broadcasted_iota(jnp.int32, (128, CHUNK), 0) == slot[...] % 128
    slot_hot = jnp.where(in_slot, 1.0, 0.0).astype(BF16)
    parts = jnp.concatenate([jnp.where(in_half, moved[m : m + 1], 0.0) for m in range(6)], axis=0)
    high, low = split(parts)
    rest = (parts - high.astype(F32) - low.astype(F32)).astype(BF16)
    spilled[...] += nt(high, slot_hot) + nt(low, slot_hot) + nt(rest, slot_hot)

    @pl.when(step == pl.num_programs(0) - 1)
    def _():
        outgoing[...] = spilled[...]


def particles(fields, records, response, cell, counts, dest, slot):
    line = pl.BlockSpec((1, CHUNK), lambda s: (0, s))
    six = pl.BlockSpec((6, CHUNK), lambda s: (0, s))
    whole = pl.BlockSpec((4, YR, NX, ZC), lambda s: (0, 0, 0, 0), pipeline_mode=pl.Buffered(1))
    return pl.pallas_call(
        particle_kernel,
        grid=(PART // CHUNK,),
        in_specs=[pl.BlockSpec(memory_space=pltpu.SMEM), whole, six, line, line, line, line],
        out_specs=[
            six,
            pl.BlockSpec((3, CELLS, ZC), lambda s: (0, 0, 0)),
            pl.BlockSpec((48, 128), lambda s: (0, 0)),
        ],
        out_shape=[
            jax.ShapeDtypeStruct((6, PART), F32),
            jax.ShapeDtypeStruct((3, CELLS, ZC), F32),
            jax.ShapeDtypeStruct((48, 128), F32),
        ],
        scratch_shapes=[pltpu.VMEM((6 * ZC, CELLS), BF16), pltpu.VMEM((48, 128), F32)],
        compiler_params=pltpu.CompilerParams(vmem_limit_bytes=56 << 20),
        cost_estimate=pl.CostEstimate(flops=26_000_000_000, bytes_accessed=5_000_000, transcendentals=0),
        name="particles",
    )(counts, fields, records, response[None], cell[None], dest[None], slot[None])


def x_kernel(viscous, base, fields, speed, deposit, out, matrix):
    c = pl.program_id(0)

    @pl.when(c == 0)
    def _():
        for kind in range(2):
            for i in range(4):
                rows = pl.ds((kind * 4 + i) * 128, 128)
                for j in range(4):
                    block = (slice(kind * 128, (kind + 1) * 128), slice(((j - i) % 4) * 128, ((j - i) % 4 + 1) * 128))
                    high, low = base[(0,) + block], base[(1,) + block]
                    matrix[rows, pl.ds(j * 128, 128)] = high
                    matrix[rows, pl.ds(NX + j * 128, 128)] = high
                    matrix[rows, pl.ds(2 * NX + j * 128, 128)] = low

    value = jnp.concatenate([fields[0, y] for y in range(YR)], axis=1)
    high, low = split(value)
    result = mm(matrix[...], jnp.concatenate([high, low, high], axis=0))
    for y in range(YR):
        along, curve = result[:NX, y * ZC : (y + 1) * ZC], result[NX:, y * ZC : (y + 1) * ZC]
        add = jnp.where(c < 3, deposit[0, pl.ds(y * NX, NX), :], 0.0)
        out[0, y] = viscous[c] * curve - speed[0, y] * along + add


def x_terms(viscous, base, fields, deposit):
    block = (1, YR, NX, ZC)
    return pl.pallas_call(
        x_kernel,
        grid=(4,),
        in_specs=[
            pl.BlockSpec(memory_space=pltpu.SMEM),
            pl.BlockSpec((2, 256, NX), lambda c: (0, 0, 0)),
            pl.BlockSpec(block, lambda c: (c, 0, 0, 0)),
            pl.BlockSpec(block, lambda c: (0, 0, 0, 0)),
            pl.BlockSpec((1, CELLS, ZC), lambda c: (jnp.minimum(c, 2), 0, 0)),
        ],
        out_specs=pl.BlockSpec(block, lambda c: (c, 0, 0, 0)),
        out_shape=jax.ShapeDtypeStruct((4, YR, NX, ZC), F32),
        scratch_shapes=[pltpu.VMEM((2 * NX, 3 * NX), BF16)],
        compiler_params=pltpu.CompilerParams(vmem_limit_bytes=48 << 20),
        cost_estimate=pl.CostEstimate(flops=3_300_000_000, bytes_accessed=8_000_000, transcendentals=0),
        name="x_terms",
    )(viscous, base, fields, fields, deposit)


def y_kernel(viscous, matrix, value, speed, out):
    c = pl.program_id(0)
    wide = jnp.concatenate([value[:, 0, x, :] for x in range(XB)], axis=1)
    high, low = split(wide)
    result = mm(matrix[...], jnp.concatenate([high, low, high], axis=0))
    for x in range(XB):
        along, curve = result[:NY, x * ZC : (x + 1) * ZC], result[NY:, x * ZC : (x + 1) * ZC]
        out[:, 0, x, :] = viscous[c] * curve - speed[:, 0, x, :] * along


def y_terms(viscous, matrix, value):
    block = (NY, 1, XB, ZC)
    return pl.pallas_call(
        y_kernel,
        grid=(4,),
        in_specs=[
            pl.BlockSpec(memory_space=pltpu.SMEM),
            pl.BlockSpec((2 * NY, 3 * NY), lambda c: (0, 0)),
            pl.BlockSpec(block, lambda c: (0, c, 0, 0)),
            pl.BlockSpec(block, lambda c: (0, 1, 0, 0)),
        ],
        out_specs=pl.BlockSpec(block, lambda c: (0, c, 0, 0)),
        out_shape=jax.ShapeDtypeStruct((NY, 4, XB, ZC), F32),
        compiler_params=pltpu.CompilerParams(vmem_limit_bytes=32 << 20),
        cost_estimate=pl.CostEstimate(flops=800_000_000, bytes_accessed=5_000_000, transcendentals=0),
        name="y_terms",
    )(viscous, matrix, value, value)


def z_kernel(viscous, base, value, speed, out, matrix):
    c = pl.program_id(0)

    @pl.when(c == 0)
    def _():
        for kind in range(2):
            for i in range(4):
                rows = i * 128
                for j in range(4):
                    columns = pl.ds((kind * 4 + j) * 128, 128)
                    block = (slice(kind * 128, (kind + 1) * 128), slice(((j - i) % 4) * 128, ((j - i) % 4 + 1) * 128))
                    high, low = base[(0,) + block], base[(1,) + block]
                    matrix[pl.ds(rows, 128), columns] = high
                    matrix[pl.ds(NZ + rows, 128), columns] = high
                    matrix[pl.ds(2 * NZ + rows, 128), columns] = low

    wide = jnp.concatenate([value[p, 0].reshape(YR * 128, ZC) for p in range(COLS)], axis=1)
    high, low = split(wide)
    result = mm(jnp.concatenate([high, low, high], axis=1), matrix[...])
    for q in range(COLS):
        along, curve = result[:, q * ZC : (q + 1) * ZC], result[:, NZ + q * ZC : NZ + (q + 1) * ZC]
        speed_q = speed[q, 0].reshape(YR * 128, ZC)
        out[q, 0] = (viscous[c] * curve - speed_q * along).reshape(YR, 128, ZC)


def z_terms(viscous, base, value):
    block = (COLS, 1, YR, 128, ZC)
    return pl.pallas_call(
        z_kernel,
        grid=(4,),
        in_specs=[
            pl.BlockSpec(memory_space=pltpu.SMEM),
            pl.BlockSpec((2, 256, NZ), lambda c: (0, 0, 0)),
            pl.BlockSpec(block, lambda c: (0, c, 0, 0, 0)),
            pl.BlockSpec(block, lambda c: (0, 2, 0, 0, 0)),
        ],
        out_specs=pl.BlockSpec(block, lambda c: (0, c, 0, 0, 0)),
        out_shape=jax.ShapeDtypeStruct((COLS, 4, YR, 128, ZC), F32),
        scratch_shapes=[pltpu.VMEM((3 * NZ, 2 * NZ), BF16)],
        compiler_params=pltpu.CompilerParams(vmem_limit_bytes=48 << 20),
        cost_estimate=pl.CostEstimate(flops=3_300_000_000, bytes_accessed=6_000_000, transcendentals=0),
        name="z_terms",
    )(viscous, base, value, value)


def sum_kernel(x_part, y_part, z_part, out):
    for y in range(YR):
        for q in range(COLS):
            rows = pl.ds(q * 128, 128)
            from_y = y_part[pl.ds(q * 16, 16), y, 0].reshape(128, ZC)
            out[0, y, rows, :] = x_part[0, y, rows, :] + from_y + z_part[q, 0, y]


def total(x_part, y_part, z_part):
    block = (1, YR, NX, ZC)
    return pl.pallas_call(
        sum_kernel,
        grid=(4,),
        in_specs=[
            pl.BlockSpec(block, lambda c: (c, 0, 0, 0)),
            pl.BlockSpec((ROWS, YR, 1, XB, ZC), lambda c: (0, 0, c, 0, 0)),
            pl.BlockSpec((COLS, 1, YR, 128, ZC), lambda c: (0, c, 0, 0, 0)),
        ],
        out_specs=pl.BlockSpec(block, lambda c: (c, 0, 0, 0)),
        out_shape=jax.ShapeDtypeStruct((4, YR, NX, ZC), F32),
        compiler_params=pltpu.CompilerParams(vmem_limit_bytes=32 << 20),
        cost_estimate=pl.CostEstimate(flops=2_000_000, bytes_accessed=8_000_000, transcendentals=0),
        name="total",
    )(x_part, y_part, z_part)


def swap(block, axis):
    return lax.all_to_all(block, axis, split_axis=0, concat_axis=0, tiled=True)


def on_device(fields, diffusivity, records, response_time, cell_index, counts, destination, slot):
    x_base, y_matrix, z_base = (jnp.asarray(m) for m in constants())
    to_y = fields.reshape(4, YR, ROWS, XB, ZC).transpose(2, 1, 0, 3, 4)
    to_z = fields.reshape(4, YR, COLS, 128, ZC).transpose(2, 0, 1, 3, 4)
    at_z = swap(to_z, "col")
    at_y = swap(to_y, "row")
    kept, deposit, outgoing = particles(
        fields, records, response_time, cell_index, counts, destination, slot
    )
    x_part = x_terms(diffusivity, x_base, fields, deposit)
    y_out = y_terms(diffusivity, y_matrix, at_y.reshape(NY, 4, XB, ZC))
    y_part = swap(y_out.reshape(ROWS, YR, 4, XB, ZC), "row")
    z_part = swap(z_terms(diffusivity, z_base, at_z), "col")
    tendency = total(x_part, y_part, z_part)
    outgoing = outgoing.reshape(6, 4, MIG)
    received = []
    for direction, step in ((0, 1), (1, -1)):
        pairs = [(r, r + step) for r in range(ROWS) if 0 <= r + step < ROWS]
        received.append(lax.ppermute(outgoing[:, direction], "row", pairs))
    for direction, step in ((2, 1), (3, -1)):
        pairs = [(c, (c + step) % COLS) for c in range(COLS)]
        received.append(lax.ppermute(outgoing[:, direction], "col", pairs))
    return tendency, kept, jnp.stack(received, axis=0)


def solution(mesh):
    both = ("row", "col")
    return jax.shard_map(
        on_device,
        mesh=mesh,
        in_specs=(
            P(None, "row", None, "col"),
            P(),
            P(None, both),
            P(both),
            P(both),
            P(both),
            P(both),
            P(both),
        ),
        out_specs=(P(None, "row", None, "col"), P(None, both), P(None, None, both)),
        check_vma=False,
    )
```

time: 1110 us -> 229 us (0.21); the launches traced: 1090 us -> 227 us
  other arithmetic: 504 us -> 0.01 us
  local copies, waits for them, and re-layouts: 281 us -> 17.6 us
  loops' own time: 125 us -> 0 us
  waiting for transfers between devices: 34.6 us -> 111 us
  Pallas kernels: 0 us -> 58.9 us
  matrix products: 47.3 us -> 0 us
  between operations: 44 us -> 1.48 us
  starting transfers between devices: 57.9 us -> 37.9 us
    scatter-add x5 -> x0, other arithmetic: 181 us -> none  [the longest x3 128 us: on_device(): deposit = jnp.zeros_like(flat_speed).at[:, cell_index].add(force).reshape...]
    another operation x3 -> x0, loops' own time: 125 us -> none  [the longest x2 125 us: wall_compact(): lax.linalg.tridiagonal_solve(lower, middle, upper, rhs.astype(jnp.float32))]
    gather x2 -> x0, local copies, waits for them, and re-layouts: 121 us -> none  [on_device(): fluid = jnp.take(flat_speed, cell_index, axis=1)]
    another operation x18 -> x1, other arithmetic: 121 us -> 0.01 us  [on_device(): return (tendency, kept, jnp.stack(received, axis=0))]
    div x6 -> x0, other arithmetic: 81.1 us -> none  [the longest x4 80.3 us: wall_compact(): lax.linalg.tridiagonal_solve(lower, middle, upper, rhs.astype(jnp.float32))]
    all_to_all x4, waiting for transfers between devices: 34.6 us -> 111 us  [swap(): return lax.all_to_all(block, axis, split_axis=0, concat_axis=0, tiled=True)]
    sub x4 -> x0, other arithmetic: 61.5 us -> none  [the longest x3 61 us: wall_compact(): lax.linalg.tridiagonal_solve(lower, middle, upper, rhs.astype(jnp.float32))]
    pallas_call x0 -> x5, Pallas kernels: none -> 58.9 us  [the longest x1 38.5 us: particles(): pl.pallas_call(particle_kernel, grid=(PART // CHUNK,), in_specs=[pl.Block...]
  transfers between devices with their start and end apart: 8 -> 8, of which waited for: 2 -> 3; matrix products, arithmetic and copies ran while one was open for 75% -> 2% of each run, Pallas kernels for 0% -> 24%
where the time goes in v1:
time: 229 us; the launch traced here: 227 us
  waiting for transfers between devices  111 us (48%)
  Pallas kernels  58.9 us (26%)
  starting transfers between devices  37.9 us (17%)
  local copies, waits for them, and re-layouts  17.6 us (8%)
    all_to_all x4, waiting for transfers between devices, swap(): return lax.all_to_all(block, axis, split_axis=0, concat_axis=0, tiled=True)  111 us
    pallas_call x1, Pallas kernels, particles(): pl.pallas_call(particle_kernel, grid=(PART // CHUNK,), in_specs=[pl.Block...  38.5 us
    all_to_all x4, starting transfers between devices, swap(): return lax.all_to_all(block, axis, split_axis=0, concat_axis=0, tiled=True)  28 us
    unnamed x27, local copies, waits for them, and re-layouts  10.5 us
    ppermute x2, starting transfers between devices, on_device(): received.append(lax.ppermute(outgoing[:, direction], 'row', pairs))  6.82 us
    pallas_call x1, Pallas kernels, x_terms(): pl.pallas_call(x_kernel, grid=(4,), in_specs=[pl.BlockSpec(memory_space=p...  5.83 us
    pallas_call x1, Pallas kernels, z_terms(): pl.pallas_call(z_kernel, grid=(4,), in_specs=[pl.BlockSpec(memory_space=p...  5.34 us
    pallas_call x1, Pallas kernels, y_terms(): pl.pallas_call(y_kernel, grid=(4,), in_specs=[pl.BlockSpec(memory_space=p...  5.15 us
  transfers between devices with their start and end apart: 8, of which 3 were waited for; matrix products, arithmetic and copies ran while one was open for 2% of the time, Pallas kernels for 24%

profile of v1, /device:TPU:2, one launch (start us, length us, event | category | flops | bytes accessed | tf_op | source)
XLA Modules:
  0.0 226.7 jit_solution(9737131226475941442)
XLA Ops:
  0.6 3.2 %copy.36 = f32[4,2,4,128,128]{4,3,1,0,2:T(8,128)} copy(f32[4,2,4,128,128]{4,3,2,1,0:T(8,128)} %bitcast.34) | data formatting | bytes 4194304 | tf_op jit(solution)/shard_map/reshape | solution.py:311
  3.8 8.5 %all-to-all-start.2 = ((f32[4,4,2,128,128]{4,3,2,1,0:T(8,128)}), f32[4,4,2,128,128]{4,3,2,1,0:T(8,128)S(1)}, u32[]{:S(2)}, u32[]{:S(2)}) async-start(f32[4,4,2,128,128]{4,3,2,1,0:T(8,128)} %bitcast.35), calls=%async_computation.2 | async-start | bytes 4194304 | tf_op jit(solution)/shard_map/all_to_all | solution.py:305
  12.2 3.2 %copy_bitcast_fusion.1 = f32[64,2,4,8,128]{4,3,2,1,0:T(8,128)} fusion(f32[4,2,512,128]{3,2,1,0:T(8,128)} %speed.1), kind=kLoop, calls=%fused_computation.1 | loop fusion | bytes 4194304 | tf_op jit(solution)/shard_map/transpose | solution.py:310
  15.4 0.0 copy-start.7
  15.4 0.0 copy-start.9
  15.5 47.6 %all-to-all-done.2.value.speed = f32[4,4,2,128,128]{4,3,2,1,0:T(8,128)S(1)} async-done(((f32[4,4,2,128,128]{4,3,2,1,0:T(8,128)}), f32[4,4,2,128,128]{4,3,2,1,0:T(8,128)S(1)}, u32[]{:S(2)}, u32[]{:S(2)}) %all-to-all-start.2) | async-done | bytes 2097184 | tf_op jit(solution)/shard_map/all_to_all | solution.py:305
  63.0 0.0 copy-start.1
  63.1 1.3 copy-done.1
  64.4 8.4 %all-to-all-start = ((f32[64,2,4,8,128]{4,3,2,1,0:T(8,128)}), f32[64,2,4,8,128]{4,3,2,1,0:T(8,128)S(1)}, u32[]{:S(2)}, u32[]{:S(2)}) async-start(f32[64,2,4,8,128]{4,3,2,1,0:T(8,128)} %copy_bitcast_fusion.1), calls=%async_computation | async-start | bytes 4194304 | tf_op jit(solution)/shard_map/all_to_all | solution.py:305
  72.8 0.0 copy-done.7
  72.8 0.0 copy-done.9
  72.8 0.0 copy-start.2
  72.9 1.6 copy-done.2
  74.4 5.3 %z_terms.1 = f32[4,4,2,128,128]{4,3,2,1,0:T(8,128)S(1)} custom-call(f32[4]{0:T(128)S(1)} %copy-done.7, bf16[2,256,512]{2,1,0:T(8,128)(2,1)S(1)} %copy-done.9, f32[4,4,2,128,128]{4,3,2,1,0:T(8,128)S(1)} %copy-done.2, f32[4,4,2,128,128]{4,3,2,1,0:T(8,128)S(1)} %copy-done.2), custom_call_target="tpu_custom_call" | custom-call | flops 3300000000 | bytes 6000000 | tf_op jit(solution)/shard_map/z_terms/pallas_call | solution.py:260
  79.8 0.0 copy-start.3
  79.8 1.3 copy-done.3
  81.1 0.0 copy-start.6
  81.1 19.4 %all-to-all-done = f32[64,2,4,8,128]{4,3,2,1,0:T(8,128)S(1)} async-done(((f32[64,2,4,8,128]{4,3,2,1,0:T(8,128)}), f32[64,2,4,8,128]{4,3,2,1,0:T(8,128)S(1)}, u32[]{:S(2)}, u32[]{:S(2)}) %all-to-all-start) | async-done | bytes 2097184 | tf_op jit(solution)/shard_map/all_to_all | solution.py:305
  100.5 4.5 %all-to-all-start.3 = ((f32[4,4,2,128,128]{4,3,2,1,0:T(8,128)}), f32[4,4,2,128,128]{4,3,2,1,0:T(8,128)}, u32[]{:S(2)}, u32[]{:S(2)}) async-start(f32[4,4,2,128,128]{4,3,2,1,0:T(8,128)} %copy-done.3), calls=%async_computation.3 | async-start | bytes 4194304 | tf_op jit(solution)/shard_map/all_to_all | solution.py:305
  105.0 0.0 copy-done.6
  105.0 5.2 %y_terms.1 = f32[128,4,8,128]{3,2,1,0:T(8,128)S(1)} custom-call(f32[4]{0:T(128)S(1)} %copy-done.7, bf16[256,384]{1,0:T(8,128)(2,1)S(1)} %copy-done.6, f32[128,4,8,128]{3,2,1,0:T(8,128)S(1)} %bitcast.31, f32[128,4,8,128]{3,2,1,0:T(8,128)S(1)} %bitcast.32), custom_call_target="tpu_custom_call" | custom-call | flops 800000000 | bytes 5000000 | tf_op jit(solution)/shard_map/y_terms/pallas_call | solution.py:216
  110.1 0.0 copy-start
  110.1 1.3 copy-done
  111.5 43.8 %all-to-all-done.3.z_part = f32[4,4,2,128,128]{4,3,2,1,0:T(8,128)} async-done(((f32[4,4,2,128,128]{4,3,2,1,0:T(8,128)}), f32[4,4,2,128,128]{4,3,2,1,0:T(8,128)}, u32[]{:S(2)}, u32[]{:S(2)}) %all-to-all-start.3) | async-done | bytes 2097184 | tf_op jit(solution)/shard_map/all_to_all | solution.py:305
  155.3 6.7 %all-to-all-start.1 = ((f32[64,2,4,8,128]{4,3,2,1,0:T(8,128)}), f32[64,2,4,8,128]{4,3,2,1,0:T(8,128)S(1)}, u32[]{:S(2)}, u32[]{:S(2)}) async-start(f32[64,2,4,8,128]{4,3,2,1,0:T(8,128)} %bitcast.33), calls=%async_computation.1 | async-start | bytes 4194304 | tf_op jit(solution)/shard_map/all_to_all | solution.py:305
  162.6 0.0 copy-start.8
  162.6 38.5 %particles.1 = (f32[6,8192]{1,0:T(8,128)}, f32[3,1024,128]{2,1,0:T(8,128)}, f32[48,128]{1,0:T(8,128)}) custom-call(s32[1]{0:T(128)S(6)} %copy.41.counts, f32[4,2,512,128]{3,2,1,0:T(8,128)} %speed.1, f32[6,8192]{1,0:T(8,128)} %records.1, f32[1,8192]{1,0:T(1,128)} %bitcast.44, s32[1,8192]{1,0:T(1,128)} %bitcast.45, s32[1,8192]{1,0:T(1,128)} %bitcast.46, ...), custom_call_target="tpu_custom_call" | custom-call | flops 25999998976 | bytes 5000000 | tf_op jit(solution)/shard_map/particles/pallas_call | solution.py:138
  201.2 0.8 reshape.25
  202.0 1.1 collective-permute-start.3
  203.1 4.9 %collective-permute-start.1 = (f32[6,256]{1,0:T(8,128)S(1)}, f32[6,256]{1,0:T(8,128)S(1)}, u32[]{:S(2)}, u32[]{:S(2)}) collective-permute-start(f32[6,256]{1,0:T(8,128)S(1)} %bitcast.37), channel_id=1, source_target_pairs={{4,0},{8,4},{12,8},{16,12},{20,16},{24,20},{28,24},{32,28},{36,32}... | collective-permute-start | bytes 18440 | tf_op jit(solution)/shard_map/ppermute | solution.py:326
  208.0 2.0 collective-permute-start.2
  210.0 1.9 collective-permute-start
  211.9 0.0 copy-done.8
  211.9 0.0 copy-start.10
  211.9 1.4 copy-done.10
  213.3 5.8 %x_terms.1.x_part = f32[4,2,512,128]{3,2,1,0:T(8,128)S(1)} custom-call(f32[4]{0:T(128)S(1)} %copy-done.7, bf16[2,256,512]{2,1,0:T(8,128)(2,1)S(1)} %copy-done.8, f32[4,2,512,128]{3,2,1,0:T(8,128)} %speed.1, f32[4,2,512,128]{3,2,1,0:T(8,128)} %speed.1, f32[3,1024,128]{2,1,0:T(8,128)S(1)} %copy-done.10), custom_call_target="tpu_custom_call" | custom-call | flops 3300000000 | bytes 8000000 | tf_op jit(solution)/shard_map/x_terms/pallas_call | solution.py:185
  219.2 0.0 copy-start.4
  219.2 1.3 copy-done.4
  220.5 0.0 collective-permute-done.3
  220.5 0.0 collective-permute-done.1
  220.5 0.0 collective-permute-done.2
  220.5 0.0 collective-permute-done
  220.5 0.6 copy.25
  221.1 0.0 all-to-all-done.1.y_part
  221.2 0.0 copy-start.5
  221.2 1.6 copy-done.5
  222.7 4.0 %total.1 = f32[4,2,512,128]{3,2,1,0:T(8,128)} custom-call(f32[4,2,512,128]{3,2,1,0:T(8,128)S(1)} %copy-done.5, f32[64,2,4,8,128]{4,3,2,1,0:T(8,128)S(1)} %all-to-all-done.1.y_part, f32[4,4,2,128,128]{4,3,2,1,0:T(8,128)} %all-to-all-done.3.z_part), custom_call_target="tpu_custom_call" | custom-call | flops 2000000 | bytes 8000000 | tf_op jit(solution)/shard_map/total/pallas_call | solution.py:288
  (6 shorter events, 0.0 us)
Async XLA Ops:
  3.8 59.3 %all-to-all-start.2 = ((f32[4,4,2,128,128]{4,3,2,1,0:T(8,128)}), f32[4,4,2,128,128]{4,3,2,1,0:T(8,128)S(1)}, u32[]{:S(2)}, u32[]{:S(2)}) async-start(f32[4,4,2,128,128]{4,3,2,1,0:T(8,128)} %bitcast.35), calls=%async_computation.2 | async-start | bytes 4194304 | tf_op jit(solution)/shard_map/all_to_all | solution.py:305
  15.4 57.4 %copy-start.7 = (f32[4]{0:T(128)S(1)}, f32[4]{0:T(128)}, u32[]{:S(2)}) copy-start(f32[4]{0:T(128)} %viscous.5) | copy-start | bytes 52
  15.4 57.4 %copy-start.9 = (bf16[2,256,512]{2,1,0:T(8,128)(2,1)S(1)}, bf16[2,256,512]{2,1,0:T(8,128)(2,1)}, u32[]{:S(2)}) copy-start(bf16[2,256,512]{2,1,0:T(8,128)(2,1)} %constant.8.clone.base) | copy-start | bytes 1572868
  63.0 1.3 copy-start.1
  64.4 36.1 %all-to-all-start = ((f32[64,2,4,8,128]{4,3,2,1,0:T(8,128)}), f32[64,2,4,8,128]{4,3,2,1,0:T(8,128)S(1)}, u32[]{:S(2)}, u32[]{:S(2)}) async-start(f32[64,2,4,8,128]{4,3,2,1,0:T(8,128)} %copy_bitcast_fusion.1), calls=%async_computation | async-start | bytes 4194304 | tf_op jit(solution)/shard_map/all_to_all | solution.py:305
  72.8 1.6 copy-start.2
  79.8 1.3 copy-start.3
  81.1 23.9 %copy-start.6 = (bf16[256,384]{1,0:T(8,128)(2,1)S(1)}, bf16[256,384]{1,0:T(8,128)(2,1)}, u32[]{:S(2)}) copy-start(bf16[256,384]{1,0:T(8,128)(2,1)} %constant.7.clone.matrix) | copy-start | bytes 589828
  100.5 54.8 %all-to-all-start.3 = ((f32[4,4,2,128,128]{4,3,2,1,0:T(8,128)}), f32[4,4,2,128,128]{4,3,2,1,0:T(8,128)}, u32[]{:S(2)}, u32[]{:S(2)}) async-start(f32[4,4,2,128,128]{4,3,2,1,0:T(8,128)} %copy-done.3), calls=%async_computation.3 | async-start | bytes 4194304 | tf_op jit(solution)/shard_map/all_to_all | solution.py:305
  110.1 1.3 copy-start
  155.3 65.8 %all-to-all-start.1 = ((f32[64,2,4,8,128]{4,3,2,1,0:T(8,128)}), f32[64,2,4,8,128]{4,3,2,1,0:T(8,128)S(1)}, u32[]{:S(2)}, u32[]{:S(2)}) async-start(f32[64,2,4,8,128]{4,3,2,1,0:T(8,128)} %bitcast.33), calls=%async_computation.1 | async-start | bytes 4194304 | tf_op jit(solution)/shard_map/all_to_all | solution.py:305
  162.6 49.3 %copy-start.8 = (bf16[2,256,512]{2,1,0:T(8,128)(2,1)S(1)}, bf16[2,256,512]{2,1,0:T(8,128)(2,1)}, u32[]{:S(2)}) copy-start(bf16[2,256,512]{2,1,0:T(8,128)(2,1)} %constant.6.clone.base) | copy-start | bytes 1572868
  202.0 18.5 %collective-permute-start.3 = (f32[6,256]{1,0:T(8,128)S(1)}, f32[6,256]{1,0:T(8,128)S(1)}, u32[]{:S(2)}, u32[]{:S(2)}) collective-permute-start(f32[6,256]{1,0:T(8,128)S(1)} %bitcast.36), channel_id=1, source_target_pairs={{0,3},{1,0},{2,1},{3,2},{4,7},{5,4},{6,5},{7,6},{8,11},{9,8},{10,9... | collective-permute-start | bytes 18440 | tf_op jit(solution)/shard_map/ppermute | solution.py:329
  203.1 17.4 %collective-permute-start.1 = (f32[6,256]{1,0:T(8,128)S(1)}, f32[6,256]{1,0:T(8,128)S(1)}, u32[]{:S(2)}, u32[]{:S(2)}) collective-permute-start(f32[6,256]{1,0:T(8,128)S(1)} %bitcast.37), channel_id=1, source_target_pairs={{4,0},{8,4},{12,8},{16,12},{20,16},{24,20},{28,24},{32,28},{36,32}... | collective-permute-start | bytes 18440 | tf_op jit(solution)/shard_map/ppermute | solution.py:326
  208.0 12.5 %collective-permute-start.2 = (f32[6,256]{1,0:T(8,128)S(1)}, f32[6,256]{1,0:T(8,128)S(1)}, u32[]{:S(2)}, u32[]{:S(2)}) collective-permute-start(f32[6,256]{1,0:T(8,128)S(1)} %bitcast.38), channel_id=1, source_target_pairs={{0,1},{1,2},{2,3},{3,0},{4,5},{5,6},{6,7},{7,4},{8,9},{9,10},{10,1... | collective-permute-start | bytes 18440 | tf_op jit(solution)/shard_map/ppermute | solution.py:329
  210.0 10.5 %collective-permute-start = (f32[6,256]{1,0:T(8,128)S(1)}, f32[6,256]{1,0:T(8,128)S(1)}, u32[]{:S(2)}, u32[]{:S(2)}) collective-permute-start(f32[6,256]{1,0:T(8,128)S(1)} %bitcast.39), channel_id=1, source_target_pairs={{0,4},{4,8},{8,12},{12,16},{16,20},{20,24},{24,28},{28,32},{32,36}... | collective-permute-start | bytes 18440 | tf_op jit(solution)/shard_map/ppermute | solution.py:326
  211.9 1.4 copy-start.10
  219.2 1.3 copy-start.4
  221.2 1.6 copy-start.5

commit v2 on v0

v2 whole, which is shorter than its diff:
```python
import math

import jax
import jax.numpy as jnp
import numpy as np
from jax import lax
from jax.experimental import pallas as pl
from jax.experimental.pallas import tpu as pltpu
from jax.sharding import PartitionSpec as P

F32, BF16 = jnp.float32, jnp.bfloat16
NX, NY, NZ, YR, ZC = 512, 128, 512, 2, 128
PART, MIG = 8192, 256
ROWS, COLS = 64, 4
XB = NX // ROWS
CHUNK = 1024
MESH = pl.DeviceIdType.MESH
CELLS = YR * NX
STEP, COUPLING, STRETCH = 0.2, 0.5, 1.5


def periodic_compact(n):
    eye = np.eye(n)
    up, up2 = np.roll(eye, 1, 1), np.roll(eye, 2, 1)
    lhs = eye + (up + up.T) / 3.0
    rhs = (up - up.T) * 7.0 / 9.0 + (up2 - up2.T) / 36.0
    return np.linalg.solve(lhs, rhs)


def wall_compact(n):
    lhs, rhs = np.eye(n), np.zeros((n, n))
    for j in range(1, n - 1):
        near = j in (1, n - 2)
        lhs[j, j - 1] = lhs[j, j + 1] = 0.25 if near else 1.0 / 3.0
        rhs[j, j + 1] = 0.75 if near else 7.0 / 9.0
        rhs[j, j - 1] = -rhs[j, j + 1]
        if not near:
            rhs[j, j + 2], rhs[j, j - 2] = 1.0 / 36.0, -1.0 / 36.0
    lhs[0, 1] = lhs[n - 1, n - 2] = 2.0
    rhs[0, :3] = (-2.5, 2.0, 0.5)
    rhs[n - 1, n - 3 :] = (-0.5, -2.0, 2.5)
    eta = -1.0 + 2.0 * np.arange(n) / (n - 1)
    slope = STRETCH * (1.0 - np.tanh(STRETCH * eta) ** 2) / math.tanh(STRETCH)
    return np.linalg.solve(lhs, rhs) / slope[:, None]


def spectral(n):
    offset = np.arange(n)[:, None] - np.arange(n)[None, :]
    safe = np.where(offset == 0, 1, offset)
    value = math.pi / n * (1.0 - 2.0 * (offset % 2)) / np.tan(math.pi * safe / n)
    return np.where(offset == 0, 0.0, value)


def split_np(matrix):
    high = matrix.astype(np.float32).astype(BF16)
    low = (matrix - high.astype(np.float64)).astype(np.float32).astype(BF16)
    return high, low


def split(value):
    high = value.astype(BF16)
    return high, (value - high.astype(F32)).astype(BF16)


def constants():
    dx, dy, dz = periodic_compact(NX), wall_compact(NY), spectral(NZ)
    x_row = np.concatenate([dx[:128], (dx @ dx)[:128]], 0)
    z_t = np.concatenate([dz.T[:128], (dz @ dz).T[:128]], 0)
    x_high, x_low = split_np(x_row)
    z_high, z_low = split_np(z_t)
    y_high, y_low = split_np(np.concatenate([dy, dy @ dy], 0))
    y_three = np.concatenate([y_high, y_high, y_low], 1)
    return np.stack([x_high, x_low]), y_three, np.stack([z_high, z_low])


def nt(a, b):
    return lax.dot_general(a, b, (((1,), (1,)), ((), ())), preferred_element_type=F32)


def mm(a, b):
    return jnp.dot(a, b, preferred_element_type=F32)


def expand(base, matrix, size, by_rows):
    for kind in range(2):
        for i in range(4):
            for j in range(4):
                at = ((j - i) if by_rows else (i + j)) % 4
                block = (slice(kind * 128, (kind + 1) * 128), slice(at * 128, (at + 1) * 128))
                for place, part in enumerate((0, 0, 1)):
                    tile = base[(part,) + block]
                    if by_rows:
                        matrix[pl.ds((kind * 4 + i) * 128, 128), pl.ds(place * size + j * 128, 128)] = tile
                    else:
                        matrix[pl.ds(place * size + i * 128, 128), pl.ds((kind * 4 + j) * 128, 128)] = tile


def step_kernel(
    counts, viscous, x_base, y_matrix, z_base, fields, records, response, cell, dest, slot,
    tendency, kept, arrivals,
    at_y, at_z, y_out, z_out, back_y, back_z, x_matrix, z_matrix, table, deposit, spilled, packed, landed,
    y_send, y_recv, back_y_send, back_y_recv, z_send, z_recv, back_z_send, back_z_recv, move_send, move_recv,
):
    r, c = lax.axis_index("row"), lax.axis_index("col")
    x_here = pl.ds(pl.multiple_of(c * 128, 128), 128)

    barrier = pltpu.get_barrier_semaphore()

    def greet(i, _):
        pl.semaphore_signal(barrier, inc=1, device_id=(lax.rem(r + i, ROWS), c), device_id_type=MESH)
        return 0

    lax.fori_loop(1, ROWS, greet, 0)
    for d in range(1, COLS):
        pl.semaphore_signal(barrier, inc=1, device_id=(r, lax.rem(c + d, COLS)), device_id_type=MESH)
    pl.semaphore_wait(barrier, ROWS + COLS - 2)

    def peer(i):
        half = lax.div(i + 1, 2)
        return lax.rem(r + jnp.where(lax.rem(i, 2) == 1, half, ROWS - half), ROWS)

    def to_y(p, from_row):
        return pltpu.make_async_remote_copy(
            src_ref=fields.at[:, :, pl.ds(pl.multiple_of(p * XB, XB), XB), :],
            dst_ref=at_y.at[:, pl.ds(from_row * YR, YR)],
            send_sem=y_send.at[p],
            recv_sem=y_recv.at[from_row],
            device_id=(p, c),
            device_id_type=MESH,
        )

    def from_y(p, from_row):
        return pltpu.make_async_remote_copy(
            src_ref=y_out.at[:, pl.ds(p * YR, YR)],
            dst_ref=back_y.at[:, :, pl.ds(pl.multiple_of(from_row * XB, XB), XB), :],
            send_sem=back_y_send.at[p],
            recv_sem=back_y_recv.at[from_row],
            device_id=(p, c),
            device_id_type=MESH,
        )

    def to_z(d, q):
        to = lax.rem(c + d, COLS)
        return pltpu.make_async_remote_copy(
            src_ref=fields.at[q, :, pl.ds(pl.multiple_of(to * 128, 128), 128), :],
            dst_ref=at_z.at[d - 1, q],
            send_sem=z_send.at[d, q],
            recv_sem=z_recv.at[d, q],
            device_id=(r, to),
            device_id_type=MESH,
        )

    def from_z(d, q, sender):
        return pltpu.make_async_remote_copy(
            src_ref=z_out.at[d, q],
            dst_ref=back_z.at[q, :, pl.ds(pl.multiple_of(sender * 128, 128), 128), :],
            send_sem=back_z_send.at[d, q],
            recv_sem=back_z_recv.at[d, q],
            device_id=(r, lax.rem(c + d, COLS)),
            device_id_type=MESH,
        )

    def start_z(q, _):
        for d in (1, 3, 2):
            to_z(d, q).start()
        return 0

    def start_y(i, _):
        to_y(peer(i), r).start()
        return 0

    lax.fori_loop(0, 4, start_z, 0)
    lax.fori_loop(1, ROWS, start_y, 0)
    at_y[:, pl.ds(r * YR, YR)] = fields[:, :, pl.ds(pl.multiple_of(r * XB, XB), XB), :]

    for a in range(3):
        high, low = split(fields[a].reshape(CELLS, ZC).T)
        table[pl.ds(a * ZC, ZC), :] = high
        table[pl.ds((3 + a) * ZC, ZC), :] = low
    deposit[...] = jnp.zeros_like(deposit)
    spilled[...] = jnp.zeros_like(spilled)
    expand(x_base, x_matrix, NX, True)
    expand(z_base, z_matrix, NZ, False)

    def particles(step, _):
        here = pl.ds(pl.multiple_of(step * CHUNK, CHUNK), CHUNK)
        index = cell[:, here]
        row, lane = index // ZC, index % ZC
        local = step * CHUNK + lax.broadcasted_iota(jnp.int32, (1, CHUNK), 1)
        live = local < counts[0]
        in_row = lax.broadcasted_iota(jnp.int32, (CELLS, CHUNK), 0) == row
        hot = jnp.where(in_row, 1.0, 0.0).astype(BF16)
        in_lane = lax.broadcasted_iota(jnp.int32, (ZC, CHUNK), 0) == lane
        picked = mm(table[...], hot)
        fluid = []
        for a in range(3):
            both = picked[a * ZC : (a + 1) * ZC] + picked[(3 + a) * ZC : (4 + a) * ZC]
            fluid.append(jnp.sum(jnp.where(in_lane, both, 0.0), axis=0, keepdims=True))
        fluid = jnp.concatenate(fluid, axis=0)
        speed = records[3:6, here]
        drag = (fluid - speed) / response[:, here]
        velocity = speed + STEP * drag
        moved = jnp.concatenate([records[0:3, here] + STEP * velocity, velocity], axis=0)
        to = dest[:, here]
        kept[:, here] = jnp.where(live & (to == 0), moved, 0.0)
        force = jnp.where(live, -COUPLING * drag, 0.0)
        spread = jnp.concatenate([jnp.where(in_lane, force[a : a + 1], 0.0) for a in range(3)], axis=0)
        high, low = split(spread)
        laid = nt(hot, high) + nt(hot, low)
        for a in range(3):
            deposit[a] += laid[:, a * ZC : (a + 1) * ZC]
        spot = slot[:, here]
        place = jnp.where(live & (to > 0), (to - 1) * 2 + spot // 128, 8)
        in_slot = lax.broadcasted_iota(jnp.int32, (128, CHUNK), 0) == spot % 128
        slot_hot = jnp.where(in_slot, 1.0, 0.0).astype(BF16)
        eight = jnp.concatenate([moved, jnp.zeros((2, CHUNK), F32)], axis=0)
        parts = jnp.concatenate([jnp.where(place == h, eight, 0.0) for h in range(8)], axis=0)
        high, low = split(parts)
        rest = (parts - high.astype(F32) - low.astype(F32)).astype(BF16)
        spilled[...] += nt(high, slot_hot) + nt(low, slot_hot) + nt(rest, slot_hot)
        return 0

    lax.fori_loop(0, PART // CHUNK, particles, 0)
    for d in range(4):
        for h in range(2):
            packed[d, :, pl.ds(h * 128, 128)] = spilled[pl.ds((2 * d + h) * 8, 8), :]

    def x_terms(q, _):
        value = jnp.concatenate([fields[q, y] for y in range(YR)], axis=1)
        high, low = split(value)
        result = mm(x_matrix[...], jnp.concatenate([high, low, high], axis=0))
        for y in range(YR):
            along, curve = result[:NX, y * ZC : (y + 1) * ZC], result[NX:, y * ZC : (y + 1) * ZC]
            tendency[q, y] = viscous[q] * curve - fields[0, y] * along
        return 0

    lax.fori_loop(0, 4, x_terms, 0)
    for a in range(3):
        for y in range(YR):
            tendency[a, y] += deposit[a, pl.ds(y * NX, NX), :]

    def move(d):
        target = ((lax.rem(r + 1, ROWS), c), (lax.rem(r + ROWS - 1, ROWS), c), (r, lax.rem(c + 1, COLS)), (r, lax.rem(c + 3, COLS)))[d]
        return pltpu.make_async_remote_copy(
            src_ref=packed.at[d],
            dst_ref=landed.at[d],
            send_sem=move_send.at[d],
            recv_sem=move_recv.at[d],
            device_id=target,
            device_id_type=MESH,
        )

    @pl.when(r < ROWS - 1)
    def _():
        move(0).start()

    @pl.when(r > 0)
    def _():
        move(1).start()

    move(2).start()
    move(3).start()

    def wait_y(i, _):
        p = lax.rem(r + i, ROWS)
        to_y(p, p).wait_recv()
        return 0

    lax.fori_loop(1, ROWS, wait_y, 0)

    def y_terms(q, _):
        wide = jnp.concatenate([at_y[q, :, x, :] for x in range(XB)], axis=1)
        high, low = split(wide)
        result = mm(y_matrix[...], jnp.concatenate([high, low, high], axis=0))
        for x in range(XB):
            along, curve = result[:NY, x * ZC : (x + 1) * ZC], result[NY:, x * ZC : (x + 1) * ZC]
            y_out[q, :, x, :] = viscous[q] * curve - at_y[1, :, x, :] * along
        return 0

    lax.fori_loop(0, 4, y_terms, 0)
    back_y[:, :, pl.ds(pl.multiple_of(r * XB, XB), XB), :] = y_out[:, pl.ds(r * YR, YR)]

    def start_back_y(i, _):
        from_y(peer(i), r).start()
        return 0

    lax.fori_loop(1, ROWS, start_back_y, 0)

    def z_block(q, d):
        block = fields[q, :, x_here, :] if d == 0 else at_z[d - 1, q]
        return block.reshape(YR * 128, ZC)

    for d in range(1, COLS):
        to_z(d, 2).wait_recv()

    def z_terms(q, _):
        @pl.when(q != 2)
        def _():
            for d in range(1, COLS):
                to_z(d, q).wait_recv()

        wide = jnp.concatenate([z_block(q, d) for d in range(COLS)], axis=1)
        high, low = split(wide)
        result = mm(jnp.concatenate([high, low, high], axis=1), z_matrix[...])
        for e in range(COLS):
            along, curve = result[:, e * ZC : (e + 1) * ZC], result[:, NZ + e * ZC : NZ + (e + 1) * ZC]
            term = viscous[q] * curve - z_block(2, (COLS - e) % COLS) * along
            z_out[e, q] = term.reshape(YR, 128, ZC)
        for d in (1, 3, 2):
            from_z(d, q, c).start()
        return 0

    lax.fori_loop(0, 4, z_terms, 0)
    for q in range(4):
        tendency[q, :, x_here, :] += z_out[0, q]

    def wait_back_y(i, _):
        p = lax.rem(r + i, ROWS)
        from_y(p, p).wait_recv()
        return 0

    lax.fori_loop(1, ROWS, wait_back_y, 0)

    def finish(q, _):
        tendency[q] += back_y[q]
        for d in range(1, COLS):
            sender = lax.rem(c + COLS - d, COLS)
            from_z(d, q, sender).wait_recv()
            rows = pl.ds(pl.multiple_of(sender * 128, 128), 128)
            tendency[q, :, rows, :] += back_z[q, :, rows, :]
        return 0

    lax.fori_loop(0, 4, finish, 0)

    @pl.when(r > 0)
    def _():
        move(0).wait_recv()
        arrivals[0] = landed[0, 0:6, :]

    @pl.when(r == 0)
    def _():
        arrivals[0] = jnp.zeros((6, MIG), F32)

    @pl.when(r < ROWS - 1)
    def _():
        move(1).wait_recv()
        arrivals[1] = landed[1, 0:6, :]

    @pl.when(r == ROWS - 1)
    def _():
        arrivals[1] = jnp.zeros((6, MIG), F32)

    for d in (2, 3):
        move(d).wait_recv()
        arrivals[d] = landed[d, 0:6, :]

    @pl.when(r < ROWS - 1)
    def _():
        move(0).wait_send()

    @pl.when(r > 0)
    def _():
        move(1).wait_send()

    move(2).wait_send()
    move(3).wait_send()

    def sent_y(i, _):
        p = lax.rem(r + i, ROWS)
        to_y(p, p).wait_send()
        from_y(p, p).wait_send()
        return 0

    lax.fori_loop(1, ROWS, sent_y, 0)

    def sent_z(q, _):
        for d in range(1, COLS):
            to_z(d, q).wait_send()
            from_z(d, q, c).wait_send()
        return 0

    lax.fori_loop(0, 4, sent_z, 0)


def on_device(fields, diffusivity, records, response_time, cell_index, counts, destination, slot):
    x_base, y_matrix, z_base = (jnp.asarray(m) for m in constants())
    vmem, smem = pl.BlockSpec(memory_space=pltpu.VMEM), pl.BlockSpec(memory_space=pltpu.SMEM)
    dma = pltpu.SemaphoreType.DMA
    return pl.pallas_call(
        step_kernel,
        in_specs=[smem, smem] + [vmem] * 9,
        out_specs=[vmem] * 3,
        out_shape=[
            jax.ShapeDtypeStruct((4, YR, NX, ZC), F32),
            jax.ShapeDtypeStruct((6, PART), F32),
            jax.ShapeDtypeStruct((4, 6, MIG), F32),
        ],
        scratch_shapes=[
            pltpu.VMEM((4, NY, XB, ZC), F32),
            pltpu.VMEM((COLS - 1, 4, YR, 128, ZC), F32),
            pltpu.VMEM((4, NY, XB, ZC), F32),
            pltpu.VMEM((COLS, 4, YR, 128, ZC), F32),
            pltpu.VMEM((4, YR, NX, ZC), F32),
            pltpu.VMEM((4, YR, NX, ZC), F32),
            pltpu.VMEM((2 * NX, 3 * NX), BF16),
            pltpu.VMEM((3 * NZ, 2 * NZ), BF16),
            pltpu.VMEM((6 * ZC, CELLS), BF16),
            pltpu.VMEM((3, CELLS, ZC), F32),
            pltpu.VMEM((64, 128), F32),
            pltpu.VMEM((4, 8, MIG), F32),
            pltpu.VMEM((4, 8, MIG), F32),
            dma((ROWS,)), dma((ROWS,)), dma((ROWS,)), dma((ROWS,)),
            dma((COLS, 4)), dma((COLS, 4)), dma((COLS, 4)), dma((COLS, 4)),
            dma((4,)), dma((4,)),
        ],
        compiler_params=pltpu.CompilerParams(
            collective_id=0, has_side_effects=True, vmem_limit_bytes=60 << 20
        ),
        name="whole_step",
    )(
        counts, diffusivity, x_base, y_matrix, z_base, fields, records,
        response_time[None], cell_index[None], destination[None], slot[None],
    )


def solution(mesh):
    both = ("row", "col")
    return jax.shard_map(
        on_device,
        mesh=mesh,
        in_specs=(
            P(None, "row", None, "col"),
            P(),
            P(None, both),
            P(both),
            P(both),
            P(both),
            P(both),
            P(both),
        ),
        out_specs=(P(None, "row", None, "col"), P(None, both), P(None, None, both)),
        check_vma=False,
    )
```

time: 1110 us -> 172 us (0.15); the launches traced: 1090 us -> 170 us
  other arithmetic: 504 us -> 0 us
  local copies, waits for them, and re-layouts: 281 us -> 5.19 us
  Pallas kernels: 0 us -> 164 us
  loops' own time: 125 us -> 0 us
  starting transfers between devices: 57.9 us -> 0 us
  matrix products: 47.3 us -> 0 us
  between operations: 44 us -> 1.29 us
  waiting for transfers between devices: 34.6 us -> 0 us
    scatter-add x5 -> x0, other arithmetic: 181 us -> none  [the longest x3 128 us: on_device(): deposit = jnp.zeros_like(flat_speed).at[:, cell_index].add(force).reshape...]
    pallas_call x0 -> x1, Pallas kernels: none -> 164 us  [on_device(): pl.pallas_call(step_kernel, in_specs=[smem, smem] + [vmem] * 9, out_specs...]
    another operation x3 -> x0, loops' own time: 125 us -> none  [the longest x2 125 us: wall_compact(): lax.linalg.tridiagonal_solve(lower, middle, upper, rhs.astype(jnp.float32))]
    gather x2 -> x0, local copies, waits for them, and re-layouts: 121 us -> none  [on_device(): fluid = jnp.take(flat_speed, cell_index, axis=1)]
    another operation x18 -> x0, other arithmetic: 121 us -> none  [the longest x14 78.7 us: periodic_compact(): factor = jnp.linalg.cholesky(lhs.astype(jnp.float32))]
    div x6 -> x0, other arithmetic: 81.1 us -> none  [the longest x4 80.3 us: wall_compact(): lax.linalg.tridiagonal_solve(lower, middle, upper, rhs.astype(jnp.float32))]
    sub x4 -> x0, other arithmetic: 61.5 us -> none  [the longest x3 61 us: wall_compact(): lax.linalg.tridiagonal_solve(lower, middle, upper, rhs.astype(jnp.float32))]
    slice x34 -> x0, local copies, waits for them, and re-layouts: 48.6 us -> none  [the longest x3 31.1 us: on_device(): flat_speed = fields[0:3].reshape(3, -1)]
  transfers between devices with their start and end apart: 8 -> 0, of which waited for: 2 -> 0; matrix products, arithmetic and copies ran while one was open for 75% -> 0% of each run, Pallas kernels for 0% -> 0%
where the time goes in v2:
time: 172 us; the launch traced here: 170 us
  Pallas kernels  164 us (95%)
  local copies, waits for them, and re-layouts  5.19 us (3%)
    pallas_call x1, Pallas kernels, on_device(): pl.pallas_call(step_kernel, in_specs=[smem, smem] + [vmem] * 9, out_specs...  164 us
    unnamed x4, local copies, waits for them, and re-layouts  3.81 us

profile of v2, /device:TPU:2, one launch (start us, length us, event | category | flops | bytes accessed | tf_op | source)
XLA Modules:
  0.0 170.3 jit_solution(4458459953614463310)
XLA Ops:
  1.3 163.9 %whole_step.1 = (f32[4,2,512,128]{3,2,1,0:T(8,128)}, f32[6,8192]{1,0:T(8,128)}, f32[4,6,256]{2,1,0:T(8,128)}) custom-call(s32[1]{0:T(128)S(6)} %copy.17.counts, f32[4]{0:T(128)} %viscous.1, bf16[2,256,512]{2,1,0:T(8,128)(2,1)} %constant.6.clone.x_base, bf16[256,384]{1,0:T(8,128)(2,1)} %constant.7.clone.y_matrix, bf16[2,256,512]{2,1,0:T(8,128)(2,1)} %constant.8.clone.z_base, ...), custom_call_target="tpu_custom_call" | custom-call | tf_op jit(solution)/shard_map/whole_step/pallas_call | solution.py:389
  165.2 1.4 copy.14
  166.5 0.0 copy-start
  166.5 3.1 %copy.18 = f32[4,2,512,128]{3,2,1,0:T(8,128)} copy(f32[4,2,512,128]{3,2,1,0:T(8,128)} %get-tuple-element.9) | data formatting | bytes 4194304
  169.6 0.0 copy-done
  169.6 0.7 copy.19
Async XLA Ops:
  166.5 3.1 %copy-start = (f32[6,8192]{1,0:T(8,128)S(1)}, f32[6,8192]{1,0:T(8,128)}, u32[]{:S(2)}) copy-start(f32[6,8192]{1,0:T(8,128)} %get-tuple-element.10) | copy-start | bytes 589828

commit v3 on v2

--- a/solution.py
+++ b/solution.py
@@ -12,8 +12,13 @@
 NX, NY, NZ, YR, ZC = 512, 128, 512, 2, 128
 PART, MIG = 8192, 256
 ROWS, COLS = 64, 4
-XB = NX // ROWS
+HALF = ROWS // 2
+XB = NX // HALF
+YH = NY // 2
+RANK, PAD = 28, 32
 CHUNK = 1024
+EARLY = 5
+VLIM = 46
 MESH = pl.DeviceIdType.MESH
 CELLS = YR * NX
 STEP, COUPLING, STRETCH = 0.2, 0.5, 1.5
@@ -68,9 +73,21 @@
     z_t = np.concatenate([dz.T[:128], (dz @ dz).T[:128]], 0)
     x_high, x_low = split_np(x_row)
     z_high, z_low = split_np(z_t)
-    y_high, y_low = split_np(np.concatenate([dy, dy @ dy], 0))
-    y_three = np.concatenate([y_high, y_high, y_low], 1)
-    return np.stack([x_high, x_low]), y_three, np.stack([z_high, z_low])
+    halves = [np.concatenate([np.arange(b, b + 16) for b in range(16 * k, NY, 32)]) for k in range(2)]
+    own, give = [], [None, None]
+    for k, (mine, other) in enumerate((halves, halves[::-1])):
+        both = np.concatenate([dy[mine], (dy @ dy)[mine]], 0)
+        left, scale, right = np.linalg.svd(both[:, other])
+        assert scale[RANK] < 1e-13 * scale[0]
+        reached = np.zeros((2 * YH, PAD))
+        reached[:, :RANK] = left[:, :RANK] * scale[:RANK]
+        high, low = split_np(np.concatenate([both[:, mine], reached], 1))
+        own.append(np.concatenate([high, high, low], 1))
+        wanted = np.zeros((PAD, YH))
+        wanted[:RANK] = right[:RANK]
+        high, low = split_np(wanted)
+        give[1 - k] = np.concatenate([high, high, low], 1)
+    return np.stack([x_high, x_low]), np.stack(own), np.stack(give), np.stack([z_high, z_low])
 
 
 def nt(a, b):
@@ -96,28 +113,51 @@
 
 
 def step_kernel(
-    counts, viscous, x_base, y_matrix, z_base, fields, records, response, cell, dest, slot,
+    counts, viscous, x_base, y_matrix, y_give, z_base, fields, records, response, cell, dest, slot,
     tendency, kept, arrivals,
-    at_y, at_z, y_out, z_out, back_y, back_z, x_matrix, z_matrix, table, deposit, spilled, packed, landed,
-    y_send, y_recv, back_y_send, back_y_recv, z_send, z_recv, back_z_send, back_z_recv, move_send, move_recv,
+    at_y, at_z, y_out, z_out, back_y, back_z, x_matrix, z_matrix, table, deposit, spilled, packed, landed, given, taken,
+    y_send, y_recv, back_y_send, back_y_recv, z_send, z_recv, back_z_send, back_z_recv, move_send, move_recv, give_send, give_recv,
 ):
     r, c = lax.axis_index("row"), lax.axis_index("col")
+    side = lax.rem(lax.div(r, 8), 2)
+    h = lax.div(r, 16) * 8 + lax.rem(r, 8)
+    partner = r + 8 - 16 * side
+
+    def row_of(p):
+        return lax.div(p, 8) * 16 + side * 8 + lax.rem(p, 8)
+
     x_here = pl.ds(pl.multiple_of(c * 128, 128), 128)
 
     barrier = pltpu.get_barrier_semaphore()
 
     def greet(i, _):
-        pl.semaphore_signal(barrier, inc=1, device_id=(lax.rem(r + i, ROWS), c), device_id_type=MESH)
-        return 0
-
-    lax.fori_loop(1, ROWS, greet, 0)
+        target = (row_of(lax.rem(h + i, HALF)), c)
+        pl.semaphore_signal(barrier, inc=1, device_id=target, device_id_type=MESH)
+        return 0
+
+    lax.fori_loop(1, HALF, greet, 0)
+    for row in (partner, lax.rem(r + 1, ROWS), lax.rem(r + ROWS - 1, ROWS)):
+        pl.semaphore_signal(barrier, inc=1, device_id=(row, c), device_id_type=MESH)
     for d in range(1, COLS):
         pl.semaphore_signal(barrier, inc=1, device_id=(r, lax.rem(c + d, COLS)), device_id_type=MESH)
-    pl.semaphore_wait(barrier, ROWS + COLS - 2)
+    pl.semaphore_wait(barrier, HALF - 1 + 3 + COLS - 1)
 
     def peer(i):
         half = lax.div(i + 1, 2)
-        return lax.rem(r + jnp.where(lax.rem(i, 2) == 1, half, ROWS - half), ROWS)
+        return lax.rem(h + jnp.where(lax.rem(i, 2) == 1, half, HALF - half), HALF)
+
+    def order(i):
+        return jnp.where(i == 0, 2, jnp.where(i == 3, 3, i - 1))
+
+    def give(q):
+        return pltpu.make_async_remote_copy(
+            src_ref=given.at[q, pl.ds(0, RANK)],
+            dst_ref=taken.at[q, pl.ds(0, RANK)],
+            send_sem=give_send.at[q],
+            recv_sem=give_recv.at[q],
+            device_id=(partner, c),
+            device_id_type=MESH,
+        )
 
     def to_y(p, from_row):
         return pltpu.make_async_remote_copy(
@@ -125,7 +165,7 @@
             dst_ref=at_y.at[:, pl.ds(from_row * YR, YR)],
             send_sem=y_send.at[p],
             recv_sem=y_recv.at[from_row],
-            device_id=(p, c),
+            device_id=(row_of(p), c),
             device_id_type=MESH,
         )
 
@@ -135,7 +175,7 @@
             dst_ref=back_y.at[:, :, pl.ds(pl.multiple_of(from_row * XB, XB), XB), :],
             send_sem=back_y_send.at[p],
             recv_sem=back_y_recv.at[from_row],
-            device_id=(p, c),
+            device_id=(row_of(p), c),
             device_id_type=MESH,
         )
 
@@ -160,18 +200,20 @@
             device_id_type=MESH,
         )
 
-    def start_z(q, _):
+    def start_z(i, _):
         for d in (1, 3, 2):
-            to_z(d, q).start()
+            to_z(d, order(i)).start()
         return 0
 
     def start_y(i, _):
-        to_y(peer(i), r).start()
-        return 0
-
-    lax.fori_loop(0, 4, start_z, 0)
-    lax.fori_loop(1, ROWS, start_y, 0)
-    at_y[:, pl.ds(r * YR, YR)] = fields[:, :, pl.ds(pl.multiple_of(r * XB, XB), XB), :]
+        to_y(peer(i), h).start()
+        return 0
+
+    lax.fori_loop(0, 1, start_z, 0)
+    lax.fori_loop(1, HALF, start_y, 0)
+    lax.fori_loop(1, 3, start_z, 0)
+    at_y[:, pl.ds(h * YR, YR)] = fields[:, :, pl.ds(pl.multiple_of(h * XB, XB), XB), :]
+    taken[:, pl.ds(RANK, PAD - RANK)] = jnp.zeros((4, PAD - RANK, XB, ZC), F32)
 
     for a in range(3):
         high, low = split(fields[a].reshape(CELLS, ZC).T)
@@ -214,16 +256,38 @@
         in_slot = lax.broadcasted_iota(jnp.int32, (128, CHUNK), 0) == spot % 128
         slot_hot = jnp.where(in_slot, 1.0, 0.0).astype(BF16)
         eight = jnp.concatenate([moved, jnp.zeros((2, CHUNK), F32)], axis=0)
-        parts = jnp.concatenate([jnp.where(place == h, eight, 0.0) for h in range(8)], axis=0)
+        parts = jnp.concatenate([jnp.where(place == spot_at, eight, 0.0) for spot_at in range(8)], axis=0)
         high, low = split(parts)
         rest = (parts - high.astype(F32) - low.astype(F32)).astype(BF16)
         spilled[...] += nt(high, slot_hot) + nt(low, slot_hot) + nt(rest, slot_hot)
         return 0
 
-    lax.fori_loop(0, PART // CHUNK, particles, 0)
+    lax.fori_loop(0, EARLY, particles, 0)
+
+    def wait_y(i, _):
+        p = lax.rem(h + i, HALF)
+        to_y(p, p).wait_recv()
+        return 0
+
+    lax.fori_loop(1, HALF, wait_y, 0)
+
+    def wanted(q, _):
+        wide = jnp.concatenate([at_y[q, :, x, :] for x in range(XB)], axis=1)
+        high, low = split(wide)
+        result = mm(y_give[side], jnp.concatenate([high, low, high], axis=0))
+        for x in range(XB):
+            given[q, :, x, :] = result[:, x * ZC : (x + 1) * ZC]
+        return 0
+
+    lax.fori_loop(0, 4, wanted, 0)
+    for q in range(4):
+        give(q).start()
+    lax.fori_loop(3, 4, start_z, 0)
+
+    lax.fori_loop(EARLY, PART // CHUNK, particles, 0)
     for d in range(4):
-        for h in range(2):
-            packed[d, :, pl.ds(h * 128, 128)] = spilled[pl.ds((2 * d + h) * 8, 8), :]
+        for part in range(2):
+            packed[d, :, pl.ds(part * 128, 128)] = spilled[pl.ds((2 * d + part) * 8, 8), :]
 
     def x_terms(q, _):
         value = jnp.concatenate([fields[q, y] for y in range(YR)], axis=1)
@@ -261,44 +325,14 @@
     move(2).start()
     move(3).start()
 
-    def wait_y(i, _):
-        p = lax.rem(r + i, ROWS)
-        to_y(p, p).wait_recv()
-        return 0
-
-    lax.fori_loop(1, ROWS, wait_y, 0)
-
-    def y_terms(q, _):
-        wide = jnp.concatenate([at_y[q, :, x, :] for x in range(XB)], axis=1)
-        high, low = split(wide)
-        result = mm(y_matrix[...], jnp.concatenate([high, low, high], axis=0))
-        for x in range(XB):
-            along, curve = result[:NY, x * ZC : (x + 1) * ZC], result[NY:, x * ZC : (x + 1) * ZC]
-            y_out[q, :, x, :] = viscous[q] * curve - at_y[1, :, x, :] * along
-        return 0
-
-    lax.fori_loop(0, 4, y_terms, 0)
-    back_y[:, :, pl.ds(pl.multiple_of(r * XB, XB), XB), :] = y_out[:, pl.ds(r * YR, YR)]
-
-    def start_back_y(i, _):
-        from_y(peer(i), r).start()
-        return 0
-
-    lax.fori_loop(1, ROWS, start_back_y, 0)
-
     def z_block(q, d):
         block = fields[q, :, x_here, :] if d == 0 else at_z[d - 1, q]
         return block.reshape(YR * 128, ZC)
 
-    for d in range(1, COLS):
-        to_z(d, 2).wait_recv()
-
-    def z_terms(q, _):
-        @pl.when(q != 2)
-        def _():
-            for d in range(1, COLS):
-                to_z(d, q).wait_recv()
-
+    def z_terms(i, _):
+        q = order(i)
+        for d in range(1, COLS):
+            to_z(d, q).wait_recv()
         wide = jnp.concatenate([z_block(q, d) for d in range(COLS)], axis=1)
         high, low = split(wide)
         result = mm(jnp.concatenate([high, low, high], axis=1), z_matrix[...])
@@ -310,20 +344,47 @@
             from_z(d, q, c).start()
         return 0
 
-    lax.fori_loop(0, 4, z_terms, 0)
+    lax.fori_loop(0, 3, z_terms, 0)
+
+    def y_terms(q, _):
+        give(q).wait_recv()
+        near = jnp.concatenate([at_y[q, :, x, :] for x in range(XB)], axis=1)
+        far = jnp.concatenate([taken[q, :, x, :] for x in range(XB)], axis=1)
+        high, low = split(jnp.concatenate([near, far], axis=0))
+        result = mm(y_matrix[side], jnp.concatenate([high, low, high], axis=0))
+        for x in range(XB):
+            along, curve = result[:YH, x * ZC : (x + 1) * ZC], result[YH:, x * ZC : (x + 1) * ZC]
+            y_out[q, :, x, :] = viscous[q] * curve - at_y[1, :, x, :] * along
+        return 0
+
+    lax.fori_loop(0, 4, y_terms, 0)
+    back_y[:, :, pl.ds(pl.multiple_of(h * XB, XB), XB), :] = y_out[:, pl.ds(h * YR, YR)]
+
+    def start_back_y(i, _):
+        from_y(peer(i), h).start()
+        return 0
+
+    lax.fori_loop(1, HALF, start_back_y, 0)
+    lax.fori_loop(3, 4, z_terms, 0)
     for q in range(4):
         tendency[q, :, x_here, :] += z_out[0, q]
 
     def wait_back_y(i, _):
-        p = lax.rem(r + i, ROWS)
+        p = lax.rem(h + i, HALF)
         from_y(p, p).wait_recv()
         return 0
 
-    lax.fori_loop(1, ROWS, wait_back_y, 0)
-
-    def finish(q, _):
+    lax.fori_loop(1, HALF, wait_back_y, 0)
+
+    def add_y(q, _):
         tendency[q] += back_y[q]
-        for d in range(1, COLS):
+        return 0
+
+    lax.fori_loop(0, 4, add_y, 0)
+
+    def finish(i, _):
+        q = order(i)
+        for d in (1, 3, 2):
             sender = lax.rem(c + COLS - d, COLS)
             from_z(d, q, sender).wait_recv()
             rows = pl.ds(pl.multiple_of(sender * 128, 128), 128)
@@ -335,24 +396,24 @@
     @pl.when(r > 0)
     def _():
         move(0).wait_recv()
-        arrivals[0] = landed[0, 0:6, :]
+        arrivals[:, 0, :] = landed[0, 0:6, :]
 
     @pl.when(r == 0)
     def _():
-        arrivals[0] = jnp.zeros((6, MIG), F32)
+        arrivals[:, 0, :] = jnp.zeros((6, MIG), F32)
 
     @pl.when(r < ROWS - 1)
     def _():
         move(1).wait_recv()
-        arrivals[1] = landed[1, 0:6, :]
+        arrivals[:, 1, :] = landed[1, 0:6, :]
 
     @pl.when(r == ROWS - 1)
     def _():
-        arrivals[1] = jnp.zeros((6, MIG), F32)
+        arrivals[:, 1, :] = jnp.zeros((6, MIG), F32)
 
     for d in (2, 3):
         move(d).wait_recv()
-        arrivals[d] = landed[d, 0:6, :]
+        arrivals[:, d, :] = landed[d, 0:6, :]
 
     @pl.when(r < ROWS - 1)
     def _():
@@ -366,39 +427,40 @@
     move(3).wait_send()
 
     def sent_y(i, _):
-        p = lax.rem(r + i, ROWS)
+        p = lax.rem(h + i, HALF)
         to_y(p, p).wait_send()
         from_y(p, p).wait_send()
         return 0
 
-    lax.fori_loop(1, ROWS, sent_y, 0)
+    lax.fori_loop(1, HALF, sent_y, 0)
 
     def sent_z(q, _):
         for d in range(1, COLS):
             to_z(d, q).wait_send()
             from_z(d, q, c).wait_send()
+        give(q).wait_send()
         return 0
 
     lax.fori_loop(0, 4, sent_z, 0)
 
 
 def on_device(fields, diffusivity, records, response_time, cell_index, counts, destination, slot):
-    x_base, y_matrix, z_base = (jnp.asarray(m) for m in constants())
+    x_base, y_matrix, y_give, z_base = (jnp.asarray(m) for m in constants())
     vmem, smem = pl.BlockSpec(memory_space=pltpu.VMEM), pl.BlockSpec(memory_space=pltpu.SMEM)
     dma = pltpu.SemaphoreType.DMA
-    return pl.pallas_call(
+    tendency, kept, arrivals = pl.pallas_call(
         step_kernel,
-        in_specs=[smem, smem] + [vmem] * 9,
+        in_specs=[smem, smem] + [vmem] * 10,
         out_specs=[vmem] * 3,
         out_shape=[
             jax.ShapeDtypeStruct((4, YR, NX, ZC), F32),
             jax.ShapeDtypeStruct((6, PART), F32),
-            jax.ShapeDtypeStruct((4, 6, MIG), F32),
+            jax.ShapeDtypeStruct((6, 4, MIG), F32),
         ],
         scratch_shapes=[
-            pltpu.VMEM((4, NY, XB, ZC), F32),
+            pltpu.VMEM((4, YH, XB, ZC), F32),
             pltpu.VMEM((COLS - 1, 4, YR, 128, ZC), F32),
-            pltpu.VMEM((4, NY, XB, ZC), F32),
+            pltpu.VMEM((4, YH, XB, ZC), F32),
             pltpu.VMEM((COLS, 4, YR, 128, ZC), F32),
             pltpu.VMEM((4, YR, NX, ZC), F32),
             pltpu.VMEM((4, YR, NX, ZC), F32),
@@ -409,18 +471,21 @@
             pltpu.VMEM((64, 128), F32),
             pltpu.VMEM((4, 8, MIG), F32),
             pltpu.VMEM((4, 8, MIG), F32),
-            dma((ROWS,)), dma((ROWS,)), dma((ROWS,)), dma((ROWS,)),
+            pltpu.VMEM((4, PAD, XB, ZC), F32),
+            pltpu.VMEM((4, PAD, XB, ZC), F32),
+            dma((HALF,)), dma((HALF,)), dma((HALF,)), dma((HALF,)),
             dma((COLS, 4)), dma((COLS, 4)), dma((COLS, 4)), dma((COLS, 4)),
-            dma((4,)), dma((4,)),
+            dma((4,)), dma((4,)), dma((4,)), dma((4,)),
         ],
         compiler_params=pltpu.CompilerParams(
-            collective_id=0, has_side_effects=True, vmem_limit_bytes=60 << 20
+            collective_id=0, has_side_effects=True, vmem_limit_bytes=VLIM << 20
         ),
         name="whole_step",
     )(
-        counts, diffusivity, x_base, y_matrix, z_base, fields, records,
+        counts, diffusivity, x_base, y_matrix, y_give, z_base, fields, records,
         response_time[None], cell_index[None], destination[None], slot[None],
     )
+    return tendency, kept, arrivals.transpose(1, 0, 2)
 
 
 def solution(mesh):

time: 172 us -> 142 us (0.83)
  Pallas kernels: 164 us -> 126 us
  local copies, waits for them, and re-layouts: 5.19 us -> 12.6 us
    pallas_call x1, Pallas kernels: 164 us -> 126 us  [on_device(): pl.pallas_call(step_kernel, in_specs=[smem, smem] + [vmem] * 10, out_spec...]
    unnamed x4 -> x25, local copies, waits for them, and re-layouts: 3.81 us -> 12.6 us
where the time goes in v3:
time: 142 us; the launch traced here: 140 us
  Pallas kernels  126 us (89%)
  local copies, waits for them, and re-layouts  12.6 us (9%)
    pallas_call x1, Pallas kernels, on_device(): pl.pallas_call(step_kernel, in_specs=[smem, smem] + [vmem] * 10, out_spec...  126 us
    unnamed x25, local copies, waits for them, and re-layouts  12.6 us

profile of v3, /device:TPU:2, one launch (start us, length us, event | category | flops | bytes accessed | tf_op | source)
XLA Modules:
  0.0 139.9 jit_solution(14793643224399650221)
XLA Ops:
  1.3 0.0 copy-start
  1.3 1.6 %copy-done = f32[4,2,512,128]{3,2,1,0:T(8,128)S(1)} copy-done((f32[4,2,512,128]{3,2,1,0:T(8,128)S(1)}, f32[4,2,512,128]{3,2,1,0:T(8,128)}, u32[]{:S(2)}) %copy-start) | copy-done | bytes 2097176
  2.9 0.0 copy-start.1
  2.9 1.0 copy-done.1
  3.9 0.0 copy-start.2
  3.9 1.0 copy-done.2
  5.0 0.0 copy-start.3
  5.0 0.9 copy-done.3
  5.9 0.0 copy-start.4
  5.9 0.9 copy-done.4
  6.8 0.0 copy-start.5
  6.8 0.8 copy-done.5
  7.6 0.0 copy-start.6
  7.6 0.8 copy-done.6
  8.3 0.0 copy-start.7
  8.4 0.8 copy-done.7
  9.1 0.0 copy-start.8
  9.1 0.8 copy-done.8
  9.9 0.0 copy-start.9
  9.9 0.8 copy-done.9
  10.6 0.0 copy-start.10
  10.6 0.7 copy-done.10
  11.3 126.0 %whole_step.1 = (f32[4,2,512,128]{3,2,1,0:T(8,128)S(1)}, f32[6,8192]{1,0:T(8,128)S(1)}, f32[6,4,256]{2,1,0:T(4,128)S(1)}) custom-call(s32[1]{0:T(128)S(6)} %copy.18.counts, f32[4]{0:T(128)S(1)} %copy-done.10, bf16[2,256,512]{2,1,0:T(8,128)(2,1)S(1)} %copy-done.2, bf16[2,128,288]{2,1,0:T(8,128)(2,1)S(1)} %copy-done.4, bf16[2,32,192]{2,1,0:T(8,128)(2,1)S(1)} %copy-done.9, ...), custom_call_target="tpu_custom_call" | custom-call | tf_op jit(solution)/shard_map/whole_step/pallas_call | solution.py:451
  137.3 1.3 copy.19
  138.6 0.7 copy.20
  139.3 0.6 copy.21
Async XLA Ops:
  1.3 1.6 %copy-start = (f32[4,2,512,128]{3,2,1,0:T(8,128)S(1)}, f32[4,2,512,128]{3,2,1,0:T(8,128)}, u32[]{:S(2)}) copy-start(f32[4,2,512,128]{3,2,1,0:T(8,128)} %fields.1) | copy-start | bytes 6291460
  2.9 1.0 copy-start.1
  3.9 1.0 copy-start.2
  5.0 0.9 copy-start.3
  5.9 0.9 copy-start.4
  6.8 0.8 copy-start.5
  7.6 0.8 copy-start.6
  8.3 0.8 copy-start.7
  9.1 0.8 copy-start.8
  9.9 0.8 copy-start.9
  10.6 0.7 copy-start.10

commit v4 on v3

--- a/solution.py
+++ b/solution.py
@@ -113,11 +113,21 @@
 
 
 def step_kernel(
-    counts, viscous, x_base, y_matrix, y_give, z_base, fields, records, response, cell, dest, slot,
-    tendency, kept, arrivals,
-    at_y, at_z, y_out, z_out, back_y, back_z, x_matrix, z_matrix, table, deposit, spilled, packed, landed, given, taken,
-    y_send, y_recv, back_y_send, back_y_recv, z_send, z_recv, back_z_send, back_z_recv, move_send, move_recv, give_send, give_recv,
+    *inputs_and_rest,
 ):
+    counts, inputs, rest = inputs_and_rest[0], inputs_and_rest[1:12], inputs_and_rest[12:]
+    (
+        tendency, kept, arrivals,
+        at_y, at_z, y_out, z_out, back_y, back_z, x_matrix, z_matrix, table, deposit, spilled, packed, landed,
+        given, taken,
+        viscous, x_base, y_matrix, y_give, z_base, fields, records, response, cell, dest, slot,
+        y_send, y_recv, back_y_send, back_y_recv, z_send, z_recv, back_z_send, back_z_recv, move_send, move_recv,
+        give_send, give_recv, loaded,
+    ) = rest
+    local = (viscous, x_base, y_matrix, y_give, z_base, fields, records, response, cell, dest, slot)
+    loads = [pltpu.make_async_copy(a, b, loaded.at[i]) for i, (a, b) in enumerate(zip(inputs, local))]
+    for load in loads[5:] + loads[:5]:
+        load.start()
     r, c = lax.axis_index("row"), lax.axis_index("col")
     side = lax.rem(lax.div(r, 8), 2)
     h = lax.div(r, 16) * 8 + lax.rem(r, 8)
@@ -141,6 +151,8 @@
     for d in range(1, COLS):
         pl.semaphore_signal(barrier, inc=1, device_id=(r, lax.rem(c + d, COLS)), device_id_type=MESH)
     pl.semaphore_wait(barrier, HALF - 1 + 3 + COLS - 1)
+
+    loads[5].wait()
 
     def peer(i):
         half = lax.div(i + 1, 2)
@@ -215,6 +227,8 @@
     at_y[:, pl.ds(h * YR, YR)] = fields[:, :, pl.ds(pl.multiple_of(h * XB, XB), XB), :]
     taken[:, pl.ds(RANK, PAD - RANK)] = jnp.zeros((4, PAD - RANK, XB, ZC), F32)
 
+    for load in loads[:5] + loads[6:]:
+        load.wait()
     for a in range(3):
         high, low = split(fields[a].reshape(CELLS, ZC).T)
         table[pl.ds(a * ZC, ZC), :] = high
@@ -446,11 +460,11 @@
 
 def on_device(fields, diffusivity, records, response_time, cell_index, counts, destination, slot):
     x_base, y_matrix, y_give, z_base = (jnp.asarray(m) for m in constants())
-    vmem, smem = pl.BlockSpec(memory_space=pltpu.VMEM), pl.BlockSpec(memory_space=pltpu.SMEM)
+    vmem, hbm = pl.BlockSpec(memory_space=pltpu.VMEM), pl.BlockSpec(memory_space=pltpu.HBM)
     dma = pltpu.SemaphoreType.DMA
     tendency, kept, arrivals = pl.pallas_call(
         step_kernel,
-        in_specs=[smem, smem] + [vmem] * 10,
+        in_specs=[pl.BlockSpec(memory_space=pltpu.SMEM)] + [hbm] * 11,
         out_specs=[vmem] * 3,
         out_shape=[
             jax.ShapeDtypeStruct((4, YR, NX, ZC), F32),
@@ -473,18 +487,29 @@
             pltpu.VMEM((4, 8, MIG), F32),
             pltpu.VMEM((4, PAD, XB, ZC), F32),
             pltpu.VMEM((4, PAD, XB, ZC), F32),
+            pltpu.SMEM((4,), F32),
+            pltpu.VMEM((2, 256, NX), BF16),
+            pltpu.VMEM((2, 2 * YH, 3 * (YH + PAD)), BF16),
+            pltpu.VMEM((2, PAD, 3 * YH), BF16),
+            pltpu.VMEM((2, 256, NZ), BF16),
+            pltpu.VMEM((4, YR, NX, ZC), F32),
+            pltpu.VMEM((6, PART), F32),
+            pltpu.VMEM((1, PART), F32),
+            pltpu.VMEM((1, PART), jnp.int32),
+            pltpu.VMEM((1, PART), jnp.int32),
+            pltpu.VMEM((1, PART), jnp.int32),
             dma((HALF,)), dma((HALF,)), dma((HALF,)), dma((HALF,)),
             dma((COLS, 4)), dma((COLS, 4)), dma((COLS, 4)), dma((COLS, 4)),
-            dma((4,)), dma((4,)), dma((4,)), dma((4,)),
+            dma((4,)), dma((4,)), dma((4,)), dma((4,)), dma((11,)),
         ],
         compiler_params=pltpu.CompilerParams(
             collective_id=0, has_side_effects=True, vmem_limit_bytes=VLIM << 20
         ),
         name="whole_step",
-    )(
-        counts, diffusivity, x_base, y_matrix, y_give, z_base, fields, records,
+    )(counts, *(pltpu.with_memory_space_constraint(value, pltpu.HBM) for value in (
+        diffusivity, x_base, y_matrix, y_give, z_base, fields, records,
         response_time[None], cell_index[None], destination[None], slot[None],
-    )
+    )))
     return tendency, kept, arrivals.transpose(1, 0, 2)
 
 

time: 142 us -> 131 us (0.923)
  local copies, waits for them, and re-layouts: 12.6 us -> 2.63 us
    unnamed x25 -> x3, local copies, waits for them, and re-layouts: 12.6 us -> 2.63 us
where the time goes in v4:
time: 131 us; the launch traced here: 130 us
  Pallas kernels  126 us (96%)
  local copies, waits for them, and re-layouts  2.63 us (2%)
    pallas_call x1, Pallas kernels, on_device(): pl.pallas_call(step_kernel, in_specs=[pl.BlockSpec(memory_space=pltpu.SME...  126 us
    unnamed x3, local copies, waits for them, and re-layouts  2.63 us

profile of v4, /device:TPU:2, one launch (start us, length us, event | category | flops | bytes accessed | tf_op | source)
XLA Modules:
  0.0 129.6 jit_solution(9010056858364481857)
XLA Ops:
  1.3 125.7 %whole_step.1 = (f32[4,2,512,128]{3,2,1,0:T(8,128)S(1)}, f32[6,8192]{1,0:T(8,128)S(1)}, f32[6,4,256]{2,1,0:T(4,128)S(1)}) custom-call(s32[1]{0:T(128)S(6)} %copy.18.inputs_and_rest_0_, f32[4]{0:T(128)} %inputs_and_rest_1_.1, bf16[2,256,512]{2,1,0:T(8,128)(2,1)} %constant.8.clone.inputs_and_rest_2_, bf16[2,128,288]{2,1,0:T(8,128)(2,1)} %constant.9.clone.inputs_and_rest_3_, ...), custom_call_target="tpu_custom_call" | custom-call | tf_op jit(solution)/shard_map/whole_step/pallas_call | solution.py:465
  127.0 1.3 %copy.19 = f32[4,2,512,128]{3,2,1,0:T(8,128)} copy(f32[4,2,512,128]{3,2,1,0:T(8,128)S(1)} %get-tuple-element.12) | data formatting | bytes 4194304
  128.3 0.7 copy.20
  129.0 0.6 copy.21

commit v5 on v4

--- a/solution.py
+++ b/solution.py
@@ -213,7 +213,7 @@
         )
 
     def start_z(i, _):
-        for d in (1, 3, 2):
+        for d in (2, 1, 3):
             to_z(d, order(i)).start()
         return 0
 
@@ -354,7 +354,7 @@
             along, curve = result[:, e * ZC : (e + 1) * ZC], result[:, NZ + e * ZC : NZ + (e + 1) * ZC]
             term = viscous[q] * curve - z_block(2, (COLS - e) % COLS) * along
             z_out[e, q] = term.reshape(YR, 128, ZC)
-        for d in (1, 3, 2):
+        for d in (2, 1, 3):
             from_z(d, q, c).start()
         return 0
 
@@ -398,7 +398,7 @@
 
     def finish(i, _):
         q = order(i)
-        for d in (1, 3, 2):
+        for d in (2, 1, 3):
             sender = lax.rem(c + COLS - d, COLS)
             from_z(d, q, sender).wait_recv()
             rows = pl.ds(pl.multiple_of(sender * 128, 128), 128)
@@ -456,6 +456,27 @@
         return 0
 
     lax.fori_loop(0, 4, sent_z, 0)
+
+
+def hand_kernel(*refs):
+    copies = [pltpu.make_async_copy(refs[i], refs[3 + i], refs[6].at[i]) for i in range(3)]
+    for copy in copies:
+        copy.start()
+    for copy in copies:
+        copy.wait()
+
+
+def hand_over(*values):
+    anywhere = pl.BlockSpec(memory_space=pl.ANY)
+    return pl.pallas_call(
+        hand_kernel,
+        in_specs=[anywhere] * 3,
+        out_specs=[anywhere] * 3,
+        out_shape=[jax.ShapeDtypeStruct(value.shape, F32) for value in values],
+        scratch_shapes=[pltpu.SemaphoreType.DMA((3,))],
+        compiler_params=pltpu.CompilerParams(vmem_limit_bytes=1 << 20),
+        name="hand_over",
+    )(*values)
 
 
 def on_device(fields, diffusivity, records, response_time, cell_index, counts, destination, slot):
@@ -510,6 +531,7 @@
         diffusivity, x_base, y_matrix, y_give, z_base, fields, records,
         response_time[None], cell_index[None], destination[None], slot[None],
     )))
+    tendency, kept, arrivals = hand_over(tendency, kept, arrivals)
     return tendency, kept, arrivals.transpose(1, 0, 2)
 
 

time: 131 us -> 129 us (0.985)
  local copies, waits for them, and re-layouts: 2.63 us -> 0 us
    unnamed x3 -> x0, local copies, waits for them, and re-layouts: 2.63 us -> none
    pallas_call x0 -> x1, Pallas kernels: none -> 1.42 us  [hand_over(): pl.pallas_call(hand_kernel, in_specs=[anywhere] * 3, out_specs=[anywhere]...]
where the time goes in v5:
time: 129 us
  Pallas kernels  127 us (98%)
  between operations  1.45 us (1%)
    pallas_call x1, Pallas kernels, on_device(): pl.pallas_call(step_kernel, in_specs=[pl.BlockSpec(memory_space=pltpu.SME...  126 us

profile of v5, /device:TPU:2, one launch (start us, length us, event | category | flops | bytes accessed | tf_op | source)
XLA Modules:
  0.0 128.7 jit_solution(7490785395332334795)
XLA Ops:
  1.3 125.8 %whole_step.1 = (f32[4,2,512,128]{3,2,1,0:T(8,128)S(1)}, f32[6,8192]{1,0:T(8,128)S(1)}, f32[6,4,256]{2,1,0:T(4,128)S(1)}) custom-call(s32[1]{0:T(128)S(6)} %copy.15.inputs_and_rest_0_, f32[4]{0:T(128)} %inputs_and_rest_1_.1, bf16[2,256,512]{2,1,0:T(8,128)(2,1)} %constant.8.clone.inputs_and_rest_2_, bf16[2,128,288]{2,1,0:T(8,128)(2,1)} %constant.9.clone.inputs_and_rest_3_, ...), custom_call_target="tpu_custom_call" | custom-call | tf_op jit(solution)/shard_map/whole_step/pallas_call | solution.py:486
  127.1 1.4 %hand_over.1 = (f32[4,2,512,128]{3,2,1,0:T(8,128)}, f32[6,8192]{1,0:T(8,128)}, f32[6,4,256]{2,1,0:T(4,128)}) custom-call(f32[4,2,512,128]{3,2,1,0:T(8,128)S(1)} %get-tuple-element.9.refs_0_, f32[6,8192]{1,0:T(8,128)S(1)} %get-tuple-element.10.refs_1_, f32[6,4,256]{2,1,0:T(4,128)S(1)} %get-tuple-element.11.refs_2_), custom_call_target="tpu_custom_call" | custom-call | tf_op jit(solution)/shard_map/hand_over/pallas_call | solution.py:471

commit v6 on v5

--- a/solution.py
+++ b/solution.py
@@ -18,7 +18,7 @@
 RANK, PAD = 28, 32
 CHUNK = 1024
 EARLY = 5
-VLIM = 46
+VLIM = 47
 MESH = pl.DeviceIdType.MESH
 CELLS = YR * NX
 STEP, COUPLING, STRETCH = 0.2, 0.5, 1.5
@@ -57,22 +57,39 @@
 
 
 def split_np(matrix):
-    high = matrix.astype(np.float32).astype(BF16)
-    low = (matrix - high.astype(np.float64)).astype(np.float32).astype(BF16)
-    return high, low
+    parts = []
+    for _ in range(3):
+        parts.append(matrix.astype(np.float32).astype(BF16))
+        matrix = matrix - parts[-1].astype(np.float64)
+    return parts
 
 
 def split(value):
-    high = value.astype(BF16)
-    return high, (value - high.astype(F32)).astype(BF16)
+    parts = []
+    for _ in range(3):
+        parts.append(value.astype(BF16))
+        value = value - parts[-1].astype(F32)
+    return parts
+
+
+def six(matrix, value):
+    high, middle, low = split(value)
+    size = value.shape[0]
+    result = mm(matrix[:, :size], low) + mm(matrix[:, : 2 * size], jnp.concatenate([middle] * 2, axis=0))
+    return result + mm(matrix[:, : 3 * size], jnp.concatenate([high] * 3, axis=0))
+
+
+def six_right(value, matrix):
+    high, middle, low = split(value)
+    size = value.shape[1]
+    result = mm(low, matrix[:size]) + mm(jnp.concatenate([middle] * 2, axis=1), matrix[: 2 * size])
+    return result + mm(jnp.concatenate([high] * 3, axis=1), matrix[: 3 * size])
 
 
 def constants():
     dx, dy, dz = periodic_compact(NX), wall_compact(NY), spectral(NZ)
     x_row = np.concatenate([dx[:128], (dx @ dx)[:128]], 0)
     z_t = np.concatenate([dz.T[:128], (dz @ dz).T[:128]], 0)
-    x_high, x_low = split_np(x_row)
-    z_high, z_low = split_np(z_t)
     halves = [np.concatenate([np.arange(b, b + 16) for b in range(16 * k, NY, 32)]) for k in range(2)]
     own, give = [], [None, None]
     for k, (mine, other) in enumerate((halves, halves[::-1])):
@@ -81,13 +98,11 @@
         assert scale[RANK] < 1e-13 * scale[0]
         reached = np.zeros((2 * YH, PAD))
         reached[:, :RANK] = left[:, :RANK] * scale[:RANK]
-        high, low = split_np(np.concatenate([both[:, mine], reached], 1))
-        own.append(np.concatenate([high, high, low], 1))
+        own.append(np.concatenate(split_np(np.concatenate([both[:, mine], reached], 1)), 1))
         wanted = np.zeros((PAD, YH))
         wanted[:RANK] = right[:RANK]
-        high, low = split_np(wanted)
-        give[1 - k] = np.concatenate([high, high, low], 1)
-    return np.stack([x_high, x_low]), np.stack(own), np.stack(give), np.stack([z_high, z_low])
+        give[1 - k] = np.concatenate(split_np(wanted), 1)
+    return np.stack(split_np(x_row)), np.stack(own), np.stack(give), np.stack(split_np(z_t))
 
 
 def nt(a, b):
@@ -104,7 +119,7 @@
             for j in range(4):
                 at = ((j - i) if by_rows else (i + j)) % 4
                 block = (slice(kind * 128, (kind + 1) * 128), slice(at * 128, (at + 1) * 128))
-                for place, part in enumerate((0, 0, 1)):
+                for place, part in enumerate((0, 1, 2)):
                     tile = base[(part,) + block]
                     if by_rows:
                         matrix[pl.ds((kind * 4 + i) * 128, 128), pl.ds(place * size + j * 128, 128)] = tile
@@ -230,9 +245,8 @@
     for load in loads[:5] + loads[6:]:
         load.wait()
     for a in range(3):
-        high, low = split(fields[a].reshape(CELLS, ZC).T)
-        table[pl.ds(a * ZC, ZC), :] = high
-        table[pl.ds((3 + a) * ZC, ZC), :] = low
+        for i, part in enumerate(split(fields[a].reshape(CELLS, ZC).T)):
+            table[pl.ds((3 * i + a) * ZC, ZC), :] = part
     deposit[...] = jnp.zeros_like(deposit)
     spilled[...] = jnp.zeros_like(spilled)
     expand(x_base, x_matrix, NX, True)
@@ -250,7 +264,8 @@
         picked = mm(table[...], hot)
         fluid = []
         for a in range(3):
-            both = picked[a * ZC : (a + 1) * ZC] + picked[(3 + a) * ZC : (4 + a) * ZC]
+            both = picked[(6 + a) * ZC : (7 + a) * ZC] + picked[(3 + a) * ZC : (4 + a) * ZC]
+            both = picked[a * ZC : (a + 1) * ZC] + both
             fluid.append(jnp.sum(jnp.where(in_lane, both, 0.0), axis=0, keepdims=True))
         fluid = jnp.concatenate(fluid, axis=0)
         speed = records[3:6, here]
@@ -261,8 +276,8 @@
         kept[:, here] = jnp.where(live & (to == 0), moved, 0.0)
         force = jnp.where(live, -COUPLING * drag, 0.0)
         spread = jnp.concatenate([jnp.where(in_lane, force[a : a + 1], 0.0) for a in range(3)], axis=0)
-        high, low = split(spread)
-        laid = nt(hot, high) + nt(hot, low)
+        high, middle, low = split(spread)
+        laid = nt(hot, low) + nt(hot, middle) + nt(hot, high)
         for a in range(3):
             deposit[a] += laid[:, a * ZC : (a + 1) * ZC]
         spot = slot[:, here]
@@ -271,9 +286,8 @@
         slot_hot = jnp.where(in_slot, 1.0, 0.0).astype(BF16)
         eight = jnp.concatenate([moved, jnp.zeros((2, CHUNK), F32)], axis=0)
         parts = jnp.concatenate([jnp.where(place == spot_at, eight, 0.0) for spot_at in range(8)], axis=0)
-        high, low = split(parts)
-        rest = (parts - high.astype(F32) - low.astype(F32)).astype(BF16)
-        spilled[...] += nt(high, slot_hot) + nt(low, slot_hot) + nt(rest, slot_hot)
+        high, middle, low = split(parts)
+        spilled[...] += nt(low, slot_hot) + nt(middle, slot_hot) + nt(high, slot_hot)
         return 0
 
     lax.fori_loop(0, EARLY, particles, 0)
@@ -287,8 +301,7 @@
 
     def wanted(q, _):
         wide = jnp.concatenate([at_y[q, :, x, :] for x in range(XB)], axis=1)
-        high, low = split(wide)
-        result = mm(y_give[side], jnp.concatenate([high, low, high], axis=0))
+        result = six(y_give[side], wide)
         for x in range(XB):
             given[q, :, x, :] = result[:, x * ZC : (x + 1) * ZC]
         return 0
@@ -305,17 +318,12 @@
 
     def x_terms(q, _):
         value = jnp.concatenate([fields[q, y] for y in range(YR)], axis=1)
-        high, low = split(value)
-        result = mm(x_matrix[...], jnp.concatenate([high, low, high], axis=0))
+        result = six(x_matrix, value)
         for y in range(YR):
             along, curve = result[:NX, y * ZC : (y + 1) * ZC], result[NX:, y * ZC : (y + 1) * ZC]
             tendency[q, y] = viscous[q] * curve - fields[0, y] * along
         return 0
 
-    lax.fori_loop(0, 4, x_terms, 0)
-    for a in range(3):
-        for y in range(YR):
-            tendency[a, y] += deposit[a, pl.ds(y * NX, NX), :]
 
     def move(d):
         target = ((lax.rem(r + 1, ROWS), c), (lax.rem(r + ROWS - 1, ROWS), c), (r, lax.rem(c + 1, COLS)), (r, lax.rem(c + 3, COLS)))[d]
@@ -348,8 +356,7 @@
         for d in range(1, COLS):
             to_z(d, q).wait_recv()
         wide = jnp.concatenate([z_block(q, d) for d in range(COLS)], axis=1)
-        high, low = split(wide)
-        result = mm(jnp.concatenate([high, low, high], axis=1), z_matrix[...])
+        result = six_right(wide, z_matrix)
         for e in range(COLS):
             along, curve = result[:, e * ZC : (e + 1) * ZC], result[:, NZ + e * ZC : NZ + (e + 1) * ZC]
             term = viscous[q] * curve - z_block(2, (COLS - e) % COLS) * along
@@ -364,8 +371,7 @@
         give(q).wait_recv()
         near = jnp.concatenate([at_y[q, :, x, :] for x in range(XB)], axis=1)
         far = jnp.concatenate([taken[q, :, x, :] for x in range(XB)], axis=1)
-        high, low = split(jnp.concatenate([near, far], axis=0))
-        result = mm(y_matrix[side], jnp.concatenate([high, low, high], axis=0))
+        result = six(y_matrix[side], jnp.concatenate([near, far], axis=0))
         for x in range(XB):
             along, curve = result[:YH, x * ZC : (x + 1) * ZC], result[YH:, x * ZC : (x + 1) * ZC]
             y_out[q, :, x, :] = viscous[q] * curve - at_y[1, :, x, :] * along
@@ -380,6 +386,10 @@
 
     lax.fori_loop(1, HALF, start_back_y, 0)
     lax.fori_loop(3, 4, z_terms, 0)
+    lax.fori_loop(0, 4, x_terms, 0)
+    for a in range(3):
+        for y in range(YR):
+            tendency[a, y] += deposit[a, pl.ds(y * NX, NX), :]
     for q in range(4):
         tendency[q, :, x_here, :] += z_out[0, q]
 
@@ -501,7 +511,7 @@
             pltpu.VMEM((4, YR, NX, ZC), F32),
             pltpu.VMEM((2 * NX, 3 * NX), BF16),
             pltpu.VMEM((3 * NZ, 2 * NZ), BF16),
-            pltpu.VMEM((6 * ZC, CELLS), BF16),
+            pltpu.VMEM((9 * ZC, CELLS), BF16),
             pltpu.VMEM((3, CELLS, ZC), F32),
             pltpu.VMEM((64, 128), F32),
             pltpu.VMEM((4, 8, MIG), F32),
@@ -509,10 +519,10 @@
             pltpu.VMEM((4, PAD, XB, ZC), F32),
             pltpu.VMEM((4, PAD, XB, ZC), F32),
             pltpu.SMEM((4,), F32),
-            pltpu.VMEM((2, 256, NX), BF16),
+            pltpu.VMEM((3, 256, NX), BF16),
             pltpu.VMEM((2, 2 * YH, 3 * (YH + PAD)), BF16),
             pltpu.VMEM((2, PAD, 3 * YH), BF16),
-            pltpu.VMEM((2, 256, NZ), BF16),
+            pltpu.VMEM((3, 256, NZ), BF16),
             pltpu.VMEM((4, YR, NX, ZC), F32),
             pltpu.VMEM((6, PART), F32),
             pltpu.VMEM((1, PART), F32),

time: 129 us -> 131 us (1.016); the launches traced: 129 us -> 129 us
  no operation moved by 1% of the time
where the time goes in v6:
time: 131 us; the launch traced here: 129 us
  Pallas kernels  127 us (97%)
  between operations  1.45 us (1%)
    pallas_call x1, Pallas kernels, on_device(): pl.pallas_call(step_kernel, in_specs=[pl.BlockSpec(memory_space=pltpu.SME...  126 us

profile of v6, /device:TPU:2, one launch (start us, length us, event | category | flops | bytes accessed | tf_op | source)
XLA Modules:
  0.0 128.7 jit_solution(303663391727577329)
XLA Ops:
  1.3 125.9 %whole_step.1 = (f32[4,2,512,128]{3,2,1,0:T(8,128)S(1)}, f32[6,8192]{1,0:T(8,128)S(1)}, f32[6,4,256]{2,1,0:T(4,128)S(1)}) custom-call(s32[1]{0:T(128)S(6)} %copy.15.inputs_and_rest_0_, f32[4]{0:T(128)} %inputs_and_rest_1_.1, bf16[3,256,512]{2,1,0:T(8,128)(2,1)} %constant.8.clone.inputs_and_rest_2_, bf16[2,128,288]{2,1,0:T(8,128)(2,1)} %constant.9.clone.inputs_and_rest_3_, ...), custom_call_target="tpu_custom_call" | custom-call | tf_op jit(solution)/shard_map/whole_step/pallas_call | solution.py:496
  127.1 1.4 %hand_over.1 = (f32[4,2,512,128]{3,2,1,0:T(8,128)}, f32[6,8192]{1,0:T(8,128)}, f32[6,4,256]{2,1,0:T(4,128)}) custom-call(f32[4,2,512,128]{3,2,1,0:T(8,128)S(1)} %get-tuple-element.9.refs_0_, f32[6,8192]{1,0:T(8,128)S(1)} %get-tuple-element.10.refs_1_, f32[6,4,256]{2,1,0:T(4,128)S(1)} %get-tuple-element.11.refs_2_), custom_call_target="tpu_custom_call" | custom-call | tf_op jit(solution)/shard_map/hand_over/pallas_call | solution.py:481
